TPU v7x, 1024 devices: a whole 4x8x16 slice. The times are simulated.
1024 devices in a mesh: row: 16 (over y, core), col: 64 (over z, x).
Axes of the slice: x: 4, y: 8, z: 16, core: 2. Of those that a mesh axis runs over, the one named last changes fastest.
Arguments:
- tokens: bfloat16 [1024, 8192], P('col', 'row'), may hold values from -120 to 120
- source: int32 [1024], replicated, may hold values from 0 to 1023, each once
- gain: float32 [8192], P('row'), may hold values from 0.5 to 1.5
- gate_weight: bfloat16 [8192, 29568], P('row', 'col'), may hold values from -0.0625 to 0.0625
- up_weight: bfloat16 [8192, 29568], P('row', 'col'), may hold values from -0.0625 to 0.0625
- down_weight: bfloat16 [29568, 8192], P('col', 'row'), may hold values from -0.03125 to 0.03125
Outputs:
- mixed: bfloat16 [1024, 8192], P('col', 'row')
All inputs are finite; a program needn't handle non-finite values.
Results may differ from a plain program's by a relative error of at most 0.0064.
Values may be sent and summed in bfloat16 or wider, within the bound.
No kernel may reach another device: no remote copies, remote signals or barrier semaphores. Data moves between devices by JAX's collectives and lax.ppermute only.
A program may use at most 32 MiB of HBM per device.

v0:
```python
import jax
import jax.numpy as jnp
from jax import lax
from jax.sharding import Mesh
from jax.sharding import PartitionSpec as P

D = 8192
COL = ("col_0", "col_1")


def gathered_by_axis(value, axes, dim):
    filled = value
    for number in range(len(axes) - 1, -1, -1):
        filled = lax.all_gather(filled, axes[number], axis=dim, tiled=True)
    return filled


def copy_for_each(value, axis):
    copies = jnp.broadcast_to(value, (lax.axis_size(axis), *value.shape))
    return lax.all_to_all(copies, axis, split_axis=0, concat_axis=0, tiled=True)


def over_copies(value, axis):
    everything = copy_for_each(value, axis)
    return jnp.sum(everything, axis=0)


def sent_together(arrays, axis, dim, along):
    both = jnp.concatenate(arrays, axis=along)
    filled, at, gathered = (lax.psum_scatter(both, axis, scatter_dimension=dim, tiled=True), 0, [])
    for a in arrays:
        gathered.append(lax.slice_in_dim(filled, at, at + a.shape[along], axis=along))
        at += a.shape[along]
    return tuple(gathered)


def sum_in_order(pieces, axes, sequence):
    shape = [lax.axis_size(a) for a in axes]
    pieces = pieces.reshape(*shape, *pieces.shape[1:])
    pieces = pieces.transpose(*sequence, *range(len(axes), pieces.ndim))
    pieces = pieces.reshape(-1, *pieces.shape[len(axes) :])
    for k in sequence:
        pieces = lax.psum_scatter(pieces, axes[k], scatter_dimension=0, tiled=True)
    return pieces[0]


def cut_along(value, dim, length):
    before, after = (value.shape[:dim], value.shape[dim + 1 :])
    return jnp.moveaxis(value.reshape(*before, length, -1, *after), dim, 0)


def summed_rows_2(value, axes, sequence, dim):
    length = lax.axis_size(axes)
    return sum_in_order(cut_along(value, dim, length), axes, sequence)


def activate(gate_sum, up_sum, square_sum):
    scale = lax.rsqrt(square_sum / D + 1e-06)
    return (jax.nn.silu(scale * gate_sum) * (scale * up_sum)).astype(jnp.bfloat16)


def on_device(tokens, source, gain, gate_weight, up_weight, down_weight):
    gathered = gathered_by_axis(tokens, COL, 0)
    merged = jnp.take(gathered, source, axis=0).astype(jnp.float32)
    squares = jnp.sum(merged * merged, axis=1, keepdims=True)
    square_all = over_copies(squares, "row")
    weighted = (merged * gain).astype(jnp.bfloat16)
    gate_part = jnp.dot(weighted, gate_weight, preferred_element_type=jnp.float32)
    up_part = jnp.dot(weighted, up_weight, preferred_element_type=jnp.float32)
    gate_sum, up_sum = sent_together((gate_part, up_part), "row", 0, 1)
    share = gate_sum.shape[0]
    square_sum = lax.dynamic_slice_in_dim(square_all, lax.axis_index("row") * share, share, 0)
    hidden_all = lax.all_gather(activate(gate_sum, up_sum, square_sum), "row", axis=0, tiled=True)
    mixed = summed_rows_2(
        jnp.dot(hidden_all, down_weight, preferred_element_type=jnp.float32), COL, (1, 0), 0
    )
    return mixed.astype(jnp.bfloat16)


def solution(mesh):
    finer = Mesh(mesh.devices.reshape(mesh.shape["row"], 16, 4), ("row", "col_0", "col_1"))
    placed = (P(COL, "row"), P(), P("row"), P("row", COL), P("row", COL), P(COL, "row"))
    return jax.shard_map(
        on_device, mesh=finer, in_specs=placed, out_specs=P(COL, "row"), check_vma=False
    )
```

profile of v0, /device:TPU:4, one launch (start us, length us, event | category | flops | bytes accessed | tf_op | source)
XLA Modules:
  0.0 330.1 jit_solution(2366573103741802817)
XLA Ops:
  6.5 24.0 %all_gather.9 = bf16[64,512]{1,0:T(8,128)(2,1)} all-gather(bf16[16,512]{1,0:T(8,128)(2,1)} %param.6), channel_id=1, replica_groups=mesh['row'=16,'col_0'=16,'col_1'=4] {'col_1'}, dimensions={0}, use_global_device_ids=true | all-gather | bytes 81920 | tf_op jit(solution)/shard_map/all_gather | solution.py:14
  30.5 0.0 all-gather.2.cloned.1.call-update
  30.6 0.0 reduce-scatter.10.cloned.1.call-start
  30.6 0.7 compare_and_fusion
  31.3 0.7 fusion.8
  32.0 69.5 %all-gather.2.cloned.1.call-done = bf16[1024,512]{1,0:T(8,128)(2,1)} async-done(((bf16[64,512]{1,0:T(8,128)(2,1)}), bf16[1024,512]{1,0:T(8,128)(2,1)}) %all-gather.2.cloned.1.call-update) | async-done | bytes 1048592 | tf_op jit(solution)/shard_map/all_gather | solution.py:14
  101.5 5.3 %gather_fusion = bf16[1024,512]{1,0:T(8,128)(2,1)S(1)} fusion(bf16[1024,512]{1,0:T(8,128)(2,1)} %all-gather.2.cloned.1.call-done, s32[1024]{0:T(1024)S(1)} %fusion.8), kind=kCustom, calls=%fused_computation | custom fusion | bytes 2101248 | tf_op jit(solution)/shard_map/jit(_take)/gather | solution.py:64
  106.9 0.0 copy-start.2
  106.9 0.8 fusion.4
  107.7 0.2 copy-done.2
  107.9 0.8 fusion.2
  108.8 2.5 pad_maximum_fusion
  111.3 5.2 %copy.13 = f32[1024,924]{1,0:T(8,128)} copy(f32[1024,924]{0,1:T(8,128)} %pad_maximum_fusion) | data formatting | bytes 7569408
  116.5 0.0 reduce-scatter.10.cloned.1.call-update
  116.5 0.6 fusion
  117.1 0.7 broadcast_in_dim.20
  117.7 6.8 %all-to-all-start = ((f32[16,1024,1]{1,2,0:T(1,128)}), f32[16,1024,1]{1,2,0:T(1,128)S(1)}, u32[]{:S(2)}, u32[]{:S(2)}) async-start(f32[16,1024,1]{1,2,0:T(1,128)} %broadcast_in_dim.20), calls=%async_computation | async-start | bytes 131072 | tf_op jit(solution)/shard_map/all_to_all | solution.py:20
  124.6 0.0 reduce-scatter.6.cloned.1.call-start
  124.6 7.7 %all-to-all-done = f32[16,1024,1]{1,2,0:T(1,128)S(1)} async-done(((f32[16,1024,1]{1,2,0:T(1,128)}), f32[16,1024,1]{1,2,0:T(1,128)S(1)}, u32[]{:S(2)}, u32[]{:S(2)}) %all-to-all-start) | async-done | bytes 65568 | tf_op jit(solution)/shard_map/all_to_all | solution.py:20
  132.4 0.1 reduce_sum.19
  132.4 0.1 add_rsqrt_fusion
  132.5 51.4 %reduce-scatter.10.cloned.1.call-done = f32[64,924]{1,0:T(8,128)} async-done(((f32[1024,924]{1,0:T(8,128)}), f32[64,924]{1,0:T(8,128)}) %reduce-scatter.10.cloned.1.call-update) | async-done | bytes 236560 | tf_op jit(solution)/shard_map/reduce_scatter | solution.py:30
  183.9 1.1 fusion.7
  185.0 17.6 %all_gather.11 = bf16[1024,462]{1,0:T(8,128)(2,1)S(1)} all-gather(bf16[64,462]{1,0:T(8,128)(2,1)S(1)} %fusion.7), channel_id=1, replica_groups=mesh['row'=16,'col_0'=16,'col_1'=4] {'row'}, dimensions={0}, use_global_device_ids=true | all-gather | bytes 1005312 | tf_op jit(solution)/shard_map/all_gather | solution.py:73
  202.6 0.7 fusion.9
  203.3 1.6 copy.12
  204.9 0.0 reduce-scatter.6.cloned.1.call-update
  204.9 0.0 reduce-scatter.8.cloned.1.call-start
  205.0 38.2 %reduce-scatter.6.cloned.1.call-done = f32[16,16,512]{2,1,0:T(8,128)} async-done(((f32[64,16,512]{2,1,0:T(8,128)}), f32[16,16,512]{2,1,0:T(8,128)}) %reduce-scatter.6.cloned.1.call-update) | async-done | bytes 524304 | tf_op jit(solution)/shard_map/reduce_scatter | solution.py:43
  243.1 0.0 reduce-scatter.8.cloned.1.call-update
  243.2 79.1 %reduce-scatter.8.cloned.1.call-done = f32[1,16,512]{2,1,0:T(8,128)} async-done(((f32[16,16,512]{2,1,0:T(8,128)}), f32[1,16,512]{2,1,0:T(8,128)}) %reduce-scatter.8.cloned.1.call-update) | async-done | bytes 32784 | tf_op jit(solution)/shard_map/reduce_scatter | solution.py:43
  322.2 1.4 convert_bitcast_fusion
  (7 shorter events, 0.0 us)
Async XLA Ops:
  6.5 196.1 %copy-start = (bf16[462,512]{1,0:T(8,128)(2,1)S(1)}, bf16[462,512]{1,0:T(8,128)(2,1)}, u32[]{:S(2)}) copy-start(bf16[462,512]{1,0:T(8,128)(2,1)} %param.11) | copy-start | bytes 1419268
  6.5 95.0 %all-gather.2.cloned.1.call-start = ((), (), s32[]{:S(2)}) async-start(), calls=%async_computation.4 | async-start | bytes 1114112 | tf_op jit(solution)/shard_map/all_gather | solution.py:14
  30.6 153.4 %reduce-scatter.10.cloned.1.call-start = ((), (), s32[]{:S(2)}) async-start(), calls=%async_computation.7 | async-start | bytes 4456448 | tf_op jit(solution)/shard_map/reduce_scatter | solution.py:30
  32.0 74.9 %copy-start.1 = (bf16[512,462]{0,1:T(8,128)(2,1)S(1)}, bf16[512,462]{0,1:T(8,128)(2,1)}, u32[]{:S(2)}) copy-start(bf16[512,462]{0,1:T(8,128)(2,1)} %param.9) | copy-start | bytes 1419268
  32.0 74.9 %copy-start.3 = (f32[512]{0:T(512)S(1)}, f32[512]{0:T(512)}, u32[]{:S(2)}) copy-start(f32[512]{0:T(512)} %param.8) | copy-start | bytes 6148
  106.9 1.0 copy-start.2
  117.7 14.6 %all-to-all-start = ((f32[16,1024,1]{1,2,0:T(1,128)}), f32[16,1024,1]{1,2,0:T(1,128)S(1)}, u32[]{:S(2)}, u32[]{:S(2)}) async-start(f32[16,1024,1]{1,2,0:T(1,128)} %broadcast_in_dim.20), calls=%async_computation | async-start | bytes 131072 | tf_op jit(solution)/shard_map/all_to_all | solution.py:20
  124.6 118.6 %reduce-scatter.6.cloned.1.call-start = ((), (), s32[]{:S(2)}) async-start(), calls=%async_computation.5 | async-start | bytes 2621440 | tf_op jit(solution)/shard_map/reduce_scatter | solution.py:43
  204.9 117.3 %reduce-scatter.8.cloned.1.call-start = ((), (), s32[]{:S(2)}) async-start(), calls=%async_computation.6 | async-start | bytes 557056 | tf_op jit(solution)/shard_map/reduce_scatter | solution.py:43
Sparse Core Ops, SparseCore 0:
  30.7 70.7 all-gather.1
  116.6 67.2 reduce-scatter.9
  205.0 38.0 reduce-scatter.5
  246.4 75.8 reduce-scatter.7
where the time goes:
time: 331 us; the launch traced here: 330 us
  waiting for transfers between devices  246 us (74%)
  blocking collectives  41.6 us (13%)
  between operations  13.2 us (4%)
  local copies, waits for them, and re-layouts  13 us (4%)
  other arithmetic  7.08 us (2%)
  starting transfers between devices  6.97 us (2%)
    reduce_scatter x2, waiting for transfers between devices, sum_in_order(): pieces = lax.psum_scatter(pieces, axes[k], scatter_dimension=0, tiled=True)  117 us
    all_gather x1, waiting for transfers between devices, gathered_by_axis(): filled = lax.all_gather(filled, axes[number], axis=dim, tiled=True)  69.5 us
    reduce_scatter x1, waiting for transfers between devices, sent_together(): lax.psum_scatter(both, axis, scatter_dimension=dim, tiled=True)  51.4 us
    all_gather x1, blocking collectives, gathered_by_axis(): filled = lax.all_gather(filled, axes[number], axis=dim, tiled=True)  24 us
    all_gather x1, blocking collectives, on_device(): lax.all_gather(activate(gate_sum, up_sum, square_sum), 'row', axis=0, til...  17.6 us
    all_to_all x1, waiting for transfers between devices, copy_for_each(): return lax.all_to_all(copies, axis, split_axis=0, concat_axis=0, tiled=True)  7.74 us
    all_to_all x1, starting transfers between devices, copy_for_each(): return lax.all_to_all(copies, axis, split_axis=0, concat_axis=0, tiled=True)  6.84 us
  transfers between devices with their start and end apart: 5, of which 5 were waited for; matrix products, arithmetic and copies ran while one was open for 1% of the time, Pallas kernels for 0%

commit v1 on v0

v1 whole, which is shorter than its diff:
```python
import functools

import jax
import jax.numpy as jnp
from jax import lax
from jax.experimental import pallas as pl
from jax.experimental.pallas import tpu as pltpu
from jax.sharding import Mesh
from jax.sharding import PartitionSpec as P

WIDTH = 8192
INTERPRET = False
NT = (((1,), (1,)), ((), ()))


def swapped(value, axis):
    return lax.all_to_all(value, axis, split_axis=0, concat_axis=0, tiled=True)


def copied_to_all(value, axis):
    copies = jnp.broadcast_to(value, (lax.axis_size(axis), *value.shape))
    return swapped(copies, axis).reshape(-1, *value.shape[1:])


def summed(pieces):
    return jnp.sum(pieces.astype(jnp.float32), axis=0).astype(jnp.bfloat16)


def products_kernel(sizes, other, source_ref, gathered_ref, gain_ref, gate_ref, up_ref, out_ref, pick_ref, weight_ref):
    ny, nc, nz, nx, share = sizes
    total = gathered_ref.shape[0]
    units, half = gate_ref.shape[0], weight_ref.shape[0]
    block = total // (ny * nc)
    core = lax.axis_index("c")
    wanted = nc - 1 - core if other else core
    row = lax.broadcasted_iota(jnp.int32, (share, total), 1)
    token = ((row // share % nz) * nx + row // (share * nz)) * share + row % share
    for y in range(ny):
        for k in range(block // share):
            starts = []
            for c in range(nc):
                q = (y * nc + c) * block // share + k
                starts.append((q % nz * nx + q // nz) * share)
            start = pl.multiple_of(jnp.where(wanted == 0, starts[0], starts[1]), share)
            ids = source_ref[pl.ds(start, share), :]
            at = y * block + k * share
            pick_ref[at : at + share, :] = jnp.where(ids == token, 1.0, 0.0).astype(jnp.bfloat16)
    merged = jnp.dot(pick_ref[...], gathered_ref[...], preferred_element_type=jnp.float32)
    squares = jnp.sum(merged * merged, axis=1, keepdims=True)
    weighted = (merged * gain_ref[...]).astype(jnp.bfloat16)
    weight_ref[units:, :] = jnp.zeros((half - units, weight_ref.shape[1]), jnp.bfloat16)
    weight_ref[:units, :] = gate_ref[...]
    gate = lax.dot_general(weighted, weight_ref[...], NT, preferred_element_type=jnp.float32)
    lane = lax.broadcasted_iota(jnp.int32, gate.shape, 1)
    out_ref[:, :half] = jnp.where(lane == units, squares, gate).astype(out_ref.dtype)
    weight_ref[:units, :] = up_ref[...]
    up = lax.dot_general(weighted, weight_ref[...], NT, preferred_element_type=jnp.float32)
    out_ref[:, half:] = up.astype(out_ref.dtype)


def products(sizes, other, kind, source, gathered, gain, gate_weight, up_weight):
    units, depth = gate_weight.shape
    half = -(-(units + 1) // 128) * 128
    kept = gathered.shape[0] // sizes[1]
    return pl.pallas_call(
        functools.partial(products_kernel, sizes, other),
        out_shape=jax.ShapeDtypeStruct((kept, 2 * half), kind),
        scratch_shapes=[
            pltpu.VMEM((kept, gathered.shape[0]), jnp.bfloat16),
            pltpu.VMEM((half, depth), jnp.bfloat16),
        ],
        interpret=INTERPRET,
        name="products_other" if other else "products_own",
    )(source, gathered, gain, gate_weight, up_weight)


def activate_kernel(units, pieces_ref, out_ref):
    total = jnp.sum(pieces_ref[...].astype(jnp.float32), axis=0)
    half = total.shape[1] // 2
    gate, up = total[:, :half], total[:, half:]
    scale = lax.rsqrt(gate[:, units : units + 1] / WIDTH + 1e-6)
    gate, up = scale * gate[:, :units], scale * up[:, :units]
    out_ref[...] = (gate / (1.0 + jnp.exp(-gate)) * up).astype(jnp.bfloat16)


def activate(pieces, units):
    return pl.pallas_call(
        functools.partial(activate_kernel, units),
        out_shape=jax.ShapeDtypeStruct((pieces.shape[1], units), jnp.bfloat16),
        interpret=INTERPRET,
        name="activate",
    )(pieces)


def on_device(tokens, source, gain, gate_weight, up_weight, down_weight):
    ny, nc, nz, nx = (lax.axis_size(a) for a in ("y", "c", "z", "x"))
    share, depth = tokens.shape
    sizes = (ny, nc, nz, nx, share)
    units = gate_weight.shape[1]
    gathered = copied_to_all(copied_to_all(tokens, "z"), "x")
    operands = (source[:, None], gathered, gain[None, :], gate_weight.T, up_weight.T)
    given = products(sizes, True, jnp.bfloat16, *operands)
    taken = lax.ppermute(given, "c", [(0, 1), (1, 0)])
    own = products(sizes, False, jnp.float32, *operands)
    both = (own + taken.astype(jnp.float32)).astype(jnp.bfloat16)
    pieces = swapped(both.reshape(ny, -1, both.shape[1]), "y")
    hidden = lax.all_gather(activate(pieces, units), ("y", "c"), axis=0, tiled=True)
    mixed = jnp.dot(hidden, down_weight, preferred_element_type=jnp.float32).astype(jnp.bfloat16)
    mixed = summed(swapped(mixed.reshape(nx, -1, depth), "x"))
    return summed(swapped(mixed.reshape(nz, share, depth), "z"))


def solution(mesh):
    row, col = mesh.shape["row"], mesh.shape["col"]
    finer = Mesh(mesh.devices.reshape(row // 2, 2, col // 4, 4), ("y", "c", "z", "x"))
    rows, cols = ("y", "c"), ("z", "x")
    placed = (P(cols, rows), P(), P(rows), P(rows, cols), P(rows, cols), P(cols, rows))
    return jax.shard_map(
        on_device, mesh=finer, in_specs=placed, out_specs=P(cols, rows), check_vma=False
    )
```

time: 331 us -> 172 us (0.52)
  the two profiles are of different devices: /device:TPU:4 before, /device:TPU:8 now
where the time goes in v1:
time: 172 us; the launch traced here: 171 us
  blocking collectives  138 us (80%)
  Pallas kernels  10.3 us (6%)
  waiting for transfers between devices  9.87 us (6%)
  starting transfers between devices  6.2 us (4%)
  local copies, waits for them, and re-layouts  3.9 us (2%)
  other arithmetic  2.83 us (2%)
    all_to_all x4, blocking collectives, swapped(): return lax.all_to_all(value, axis, split_axis=0, concat_axis=0, tiled=True)  119 us
    all_gather x1, blocking collectives, on_device(): lax.all_gather(activate(pieces, units), ('y', 'c'), axis=0, tiled=True)  18.7 us
    all_to_all x1, waiting for transfers between devices, swapped(): return lax.all_to_all(value, axis, split_axis=0, concat_axis=0, tiled=True)  9.87 us
    pallas_call x2, Pallas kernels, products(): pl.pallas_call(functools.partial(products_kernel, sizes, other), out_shap...  8.27 us
    all_to_all x1, starting transfers between devices, swapped(): return lax.all_to_all(value, axis, split_axis=0, concat_axis=0, tiled=True)  4.29 us
  transfers between devices with their start and end apart: 2, of which 1 were waited for; matrix products, arithmetic and copies ran while one was open for 1% of the time, Pallas kernels for 3%

profile of v1, /device:TPU:8, one launch (start us, length us, event | category | flops | bytes accessed | tf_op | source)
XLA Modules:
  0.0 171.4 jit_solution(1086409912454132784)
XLA Ops:
  0.0 0.0 copy-start
  0.0 0.0 copy-start.2
  0.0 0.8 broadcast_in_dim.13
  0.8 37.0 %all_to_all.25 = bf16[16,16,512]{2,1,0:T(8,128)(2,1)S(1)} all-to-all(bf16[16,16,512]{2,1,0:T(8,128)(2,1)S(1)} %broadcast_in_dim.13), channel_id=1, replica_groups=mesh['y'=8,'c'=2,'z'=16,'x'=4] {'z'}, dimensions={0} | all-to-all | bytes 524288 | tf_op jit(solution)/shard_map/all_to_all | solution.py:17
  37.9 1.1 broadcast_in_dim.14
  38.9 4.3 %all-to-all-start.1 = ((bf16[4,256,512]{2,1,0:T(8,128)(2,1)}), bf16[4,256,512]{2,1,0:T(8,128)(2,1)S(1)}, u32[]{:S(2)}, u32[]{:S(2)}) async-start(bf16[4,256,512]{2,1,0:T(8,128)(2,1)} %broadcast_in_dim.14), calls=%async_computation.1 | async-start | bytes 2097152 | tf_op jit(solution)/shard_map/all_to_all | solution.py:17
  43.2 0.0 copy-done.2
  43.2 1.0 copy.9.source_ref
  44.3 9.9 %all-to-all-done.1 = bf16[4,256,512]{2,1,0:T(8,128)(2,1)S(1)} async-done(((bf16[4,256,512]{2,1,0:T(8,128)(2,1)}), bf16[4,256,512]{2,1,0:T(8,128)(2,1)S(1)}, u32[]{:S(2)}, u32[]{:S(2)}) %all-to-all-start.1) | async-done | bytes 1048608 | tf_op jit(solution)/shard_map/all_to_all | solution.py:17
  54.1 0.0 copy-start.1
  54.1 1.0 copy-done.1
  55.1 4.0 %products_other.1 = bf16[512,1024]{1,0:T(8,128)(2,1)} custom-call(s32[1024,1]{1,0:T(8,128)} %copy.9.source_ref, bf16[1024,512]{1,0:T(8,128)(2,1)} %bitcast.11, f32[1,512]{1,0:T(1,128)} %bitcast.21, bf16[462,512]{1,0:T(8,128)(2,1)} %bitcast.14, bf16[462,512]{1,0:T(8,128)(2,1)} %bitcast.16), custom_call_target="tpu_custom_call" | custom-call | tf_op jit(solution)/shard_map/products_other/pallas_call | solution.py:65
  59.1 1.9 %collective-permute-start = (bf16[512,1024]{1,0:T(8,128)(2,1)}, bf16[512,1024]{1,0:T(8,128)(2,1)S(1)}, u32[]{:S(2)}, u32[]{:S(2)}) collective-permute-start(bf16[512,1024]{1,0:T(8,128)(2,1)} %products_other.1), channel_id=1, source_target_pairs={{0,64},{64,0},{1,65},{65,1},{2,66},{66,2},{3,67},{67,3},{4,68},{68... | collective-permute-start | bytes 3145736 | tf_op jit(solution)/shard_map/ppermute | solution.py:103
  61.0 4.3 %products_own.1 = f32[512,1024]{1,0:T(8,128)} custom-call(s32[1024,1]{1,0:T(8,128)} %copy.9.source_ref, bf16[1024,512]{1,0:T(8,128)(2,1)} %bitcast.12, f32[1,512]{1,0:T(1,128)} %bitcast.22, bf16[462,512]{1,0:T(8,128)(2,1)} %bitcast.15, bf16[462,512]{1,0:T(8,128)(2,1)} %bitcast.17), custom_call_target="tpu_custom_call" | custom-call | tf_op jit(solution)/shard_map/products_own/pallas_call | solution.py:65
  65.3 0.0 collective-permute-done
  65.3 1.9 %add_convert_fusion = bf16[512,1024]{1,0:T(8,128)(2,1)S(1)} fusion(f32[512,1024]{1,0:T(8,128)} %products_own.1, bf16[512,1024]{1,0:T(8,128)(2,1)S(1)} %collective-permute-done), kind=kLoop, calls=%fused_computation | loop fusion | flops 1572864 | bytes 4194304 | tf_op jit(solution)/shard_map/convert_element_type | solution.py:105
  67.2 35.4 %all_to_all.26.pieces_ref = bf16[8,64,1024]{2,1,0:T(8,128)(2,1)} all-to-all(bf16[8,64,1024]{2,1,0:T(8,128)(2,1)S(1)} %bitcast.13), channel_id=1, replica_groups=mesh['y'=8,'c'=2,'z'=16,'x'=4] {'y'}, dimensions={0} | all-to-all | bytes 2097152 | tf_op jit(solution)/shard_map/all_to_all | solution.py:17
  102.6 2.1 %activate.1 = bf16[64,462]{1,0:T(8,128)(2,1)} custom-call(bf16[8,64,1024]{2,1,0:T(8,128)(2,1)} %all_to_all.26.pieces_ref), custom_call_target="tpu_custom_call" | custom-call | tf_op jit(solution)/shard_map/activate/pallas_call | solution.py:87
  104.7 18.7 %all_gather.3 = bf16[1024,462]{1,0:T(8,128)(2,1)S(1)} all-gather(bf16[64,462]{1,0:T(8,128)(2,1)} %activate.1), channel_id=1, replica_groups=mesh['y'=8,'c'=2,'z'=16,'x'=4] {'y','c'}, dimensions={0}, use_global_device_ids=true | all-gather | bytes 1005312 | tf_op jit(solution)/shard_map/all_gather | solution.py:107
  123.4 0.0 copy-done
  123.4 0.7 convolution_convert_fusion
  124.2 18.3 %all_to_all.27 = bf16[4,256,512]{2,1,0:T(8,128)(2,1)S(1)} all-to-all(bf16[4,256,512]{2,1,0:T(8,128)(2,1)S(1)} %bitcast.20), channel_id=1, replica_groups=mesh['y'=8,'c'=2,'z'=16,'x'=4] {'x'}, dimensions={0} | all-to-all | bytes 2097152 | tf_op jit(solution)/shard_map/all_to_all | solution.py:17
  142.5 0.2 reduce_sum.24
  142.7 28.1 %all_to_all.28 = bf16[16,16,512]{2,1,0:T(8,128)(2,1)S(1)} all-to-all(bf16[16,16,512]{2,1,0:T(8,128)(2,1)S(1)} %bitcast.19), channel_id=1, replica_groups=mesh['y'=8,'c'=2,'z'=16,'x'=4] {'z'}, dimensions={0} | all-to-all | bytes 524288 | tf_op jit(solution)/shard_map/all_to_all | solution.py:17
  170.8 0.6 reduce_sum.25
Async XLA Ops:
  0.0 123.4 %copy-start = (bf16[462,512]{1,0:T(8,128)(2,1)S(1)}, bf16[462,512]{1,0:T(8,128)(2,1)}, u32[]{:S(2)}) copy-start(bf16[462,512]{1,0:T(8,128)(2,1)} %param.11) | copy-start | bytes 1419268
  0.0 43.2 %copy-start.2 = (s32[1024]{0:T(1024)S(1)}, s32[1024]{0:T(1024)}, u32[]{:S(2)}) copy-start(s32[1024]{0:T(1024)} %param.7) | copy-start | bytes 12292
  38.9 15.2 %all-to-all-start.1 = ((bf16[4,256,512]{2,1,0:T(8,128)(2,1)}), bf16[4,256,512]{2,1,0:T(8,128)(2,1)S(1)}, u32[]{:S(2)}, u32[]{:S(2)}) async-start(bf16[4,256,512]{2,1,0:T(8,128)(2,1)} %broadcast_in_dim.14), calls=%async_computation.1 | async-start | bytes 2097152 | tf_op jit(solution)/shard_map/all_to_all | solution.py:17
  54.1 1.0 copy-start.1
  59.1 6.2 %collective-permute-start = (bf16[512,1024]{1,0:T(8,128)(2,1)}, bf16[512,1024]{1,0:T(8,128)(2,1)S(1)}, u32[]{:S(2)}, u32[]{:S(2)}) collective-permute-start(bf16[512,1024]{1,0:T(8,128)(2,1)} %products_other.1), channel_id=1, source_target_pairs={{0,64},{64,0},{1,65},{65,1},{2,66},{66,2},{3,67},{67,3},{4,68},{68... | collective-permute-start | bytes 3145736 | tf_op jit(solution)/shard_map/ppermute | solution.py:103

commit v2 on v1

--- a/solution.py
+++ b/solution.py
@@ -9,6 +9,7 @@
 from jax.sharding import PartitionSpec as P
 
 WIDTH = 8192
+VM = pl.BlockSpec(memory_space=pltpu.VMEM)
 INTERPRET = False
 NT = (((1,), (1,)), ((), ()))
 
@@ -69,7 +70,7 @@
             pltpu.VMEM((kept, gathered.shape[0]), jnp.bfloat16),
             pltpu.VMEM((half, depth), jnp.bfloat16),
         ],
-        interpret=INTERPRET,
+        interpret=INTERPRET, compiler_params=pltpu.CompilerParams(vmem_limit_bytes=16 << 20), in_specs=[VM] * 5, out_specs=VM,
         name="products_other" if other else "products_own",
     )(source, gathered, gain, gate_weight, up_weight)
 
@@ -87,7 +88,7 @@
     return pl.pallas_call(
         functools.partial(activate_kernel, units),
         out_shape=jax.ShapeDtypeStruct((pieces.shape[1], units), jnp.bfloat16),
-        interpret=INTERPRET,
+        interpret=INTERPRET, compiler_params=pltpu.CompilerParams(vmem_limit_bytes=16 << 20), in_specs=[VM], out_specs=VM,
         name="activate",
     )(pieces)
 

time: 172 us -> 162 us (0.942)
  Pallas kernels: 10.3 us -> 2.84 us
  waiting for transfers between devices: 9.87 us -> 12 us
  local copies, waits for them, and re-layouts: 3.9 us -> 2.1 us
    pallas_call x2, Pallas kernels: 8.27 us -> 2.61 us  [products(): pl.pallas_call(functools.partial(products_kernel, sizes, other), out_shap...]
    pallas_call x1, Pallas kernels: 2.08 us -> 0.22 us  [activate(): pl.pallas_call(functools.partial(activate_kernel, units), out_shape=jax.S...]
  transfers between devices with their start and end apart: 2 -> 2, of which waited for: 1 -> 2; matrix products, arithmetic and copies ran while one was open for 1% -> 0% of each run, Pallas kernels for 3% -> 1%
where the time goes in v2:
time: 162 us
  blocking collectives  137 us (85%)
  waiting for transfers between devices  12 us (7%)
  starting transfers between devices  6.21 us (4%)
  Pallas kernels  2.84 us (2%)
  local copies, waits for them, and re-layouts  2.1 us (1%)
    all_to_all x4, blocking collectives, swapped(): return lax.all_to_all(value, axis, split_axis=0, concat_axis=0, tiled=True)  118 us
    all_gather x1, blocking collectives, on_device(): lax.all_gather(activate(pieces, units), ('y', 'c'), axis=0, tiled=True)  18.5 us
    all_to_all x1, waiting for transfers between devices, swapped(): return lax.all_to_all(value, axis, split_axis=0, concat_axis=0, tiled=True)  10.7 us
    all_to_all x1, starting transfers between devices, swapped(): return lax.all_to_all(value, axis, split_axis=0, concat_axis=0, tiled=True)  4.29 us
  transfers between devices with their start and end apart: 2, of which 2 were waited for; matrix products, arithmetic and copies ran while one was open for 0% of the time, Pallas kernels for 1%

profile of v2, /device:TPU:8, one launch (start us, length us, event | category | flops | bytes accessed | tf_op | source)
XLA Modules:
  0.0 162.0 jit_solution(2145968275790899321)
XLA Ops:
  0.0 0.0 copy-start
  0.0 0.0 copy-start.4
  0.0 0.8 broadcast_in_dim.13
  0.8 37.0 %all_to_all.25 = bf16[16,16,512]{2,1,0:T(8,128)(2,1)S(1)} all-to-all(bf16[16,16,512]{2,1,0:T(8,128)(2,1)S(1)} %broadcast_in_dim.13), channel_id=1, replica_groups=mesh['y'=8,'c'=2,'z'=16,'x'=4] {'z'}, dimensions={0} | all-to-all | bytes 524288 | tf_op jit(solution)/shard_map/all_to_all | solution.py:18
  37.9 0.0 copy-start.1
  37.9 0.0 copy-start.2
  37.9 0.0 copy-start.3
  37.9 1.1 broadcast_in_dim.14
  38.9 4.3 %all-to-all-start.1 = ((bf16[4,256,512]{2,1,0:T(8,128)(2,1)}), bf16[4,256,512]{2,1,0:T(8,128)(2,1)S(1)}, u32[]{:S(2)}, u32[]{:S(2)}) async-start(bf16[4,256,512]{2,1,0:T(8,128)(2,1)} %broadcast_in_dim.14), calls=%async_computation.1 | async-start | bytes 2097152 | tf_op jit(solution)/shard_map/all_to_all | solution.py:18
  43.2 0.0 copy-done.4
  43.2 0.2 copy.9.source_ref
  43.4 10.7 %all-to-all-done.1 = bf16[4,256,512]{2,1,0:T(8,128)(2,1)S(1)} async-done(((bf16[4,256,512]{2,1,0:T(8,128)(2,1)}), bf16[4,256,512]{2,1,0:T(8,128)(2,1)S(1)}, u32[]{:S(2)}, u32[]{:S(2)}) %all-to-all-start.1) | async-done | bytes 1048608 | tf_op jit(solution)/shard_map/all_to_all | solution.py:18
  54.1 0.0 copy-done.1
  54.1 0.0 copy-done.2
  54.1 0.0 copy-done.3
  54.1 1.3 products_other.1
  55.4 1.9 %collective-permute-start = (bf16[512,1024]{1,0:T(8,128)(2,1)S(1)}, bf16[512,1024]{1,0:T(8,128)(2,1)S(1)}, u32[]{:S(2)}, u32[]{:S(2)}) collective-permute-start(bf16[512,1024]{1,0:T(8,128)(2,1)S(1)} %products_other.1), channel_id=1, source_target_pairs={{0,64},{64,0},{1,65},{65,1},{2,66},{66,2},{3,67},{67,3},{4,68},{68... | collective-permute-start | bytes 3145736 | tf_op jit(solution)/shard_map/ppermute | solution.py:104
  57.4 1.3 products_own.1
  58.7 1.3 collective-permute-done
  60.0 0.4 add_convert_fusion
  60.4 34.9 %all_to_all.26.pieces_ref = bf16[8,64,1024]{2,1,0:T(8,128)(2,1)S(1)} all-to-all(bf16[8,64,1024]{2,1,0:T(8,128)(2,1)S(1)} %bitcast.19), channel_id=1, replica_groups=mesh['y'=8,'c'=2,'z'=16,'x'=4] {'y'}, dimensions={0} | all-to-all | bytes 2097152 | tf_op jit(solution)/shard_map/all_to_all | solution.py:18
  95.3 0.2 activate.1
  95.5 18.5 %all_gather.3 = bf16[1024,462]{1,0:T(8,128)(2,1)S(1)} all-gather(bf16[64,462]{1,0:T(8,128)(2,1)S(1)} %activate.1), channel_id=1, replica_groups=mesh['y'=8,'c'=2,'z'=16,'x'=4] {'y','c'}, dimensions={0}, use_global_device_ids=true | all-gather | bytes 1005312 | tf_op jit(solution)/shard_map/all_gather | solution.py:108
  114.1 0.0 copy-done
  114.1 0.7 convolution_convert_fusion
  114.8 18.3 %all_to_all.27 = bf16[4,256,512]{2,1,0:T(8,128)(2,1)S(1)} all-to-all(bf16[4,256,512]{2,1,0:T(8,128)(2,1)S(1)} %bitcast.22), channel_id=1, replica_groups=mesh['y'=8,'c'=2,'z'=16,'x'=4] {'x'}, dimensions={0} | all-to-all | bytes 2097152 | tf_op jit(solution)/shard_map/all_to_all | solution.py:18
  133.1 0.2 reduce_sum.24
  133.3 28.1 %all_to_all.28 = bf16[16,16,512]{2,1,0:T(8,128)(2,1)S(1)} all-to-all(bf16[16,16,512]{2,1,0:T(8,128)(2,1)S(1)} %bitcast.21), channel_id=1, replica_groups=mesh['y'=8,'c'=2,'z'=16,'x'=4] {'z'}, dimensions={0} | all-to-all | bytes 524288 | tf_op jit(solution)/shard_map/all_to_all | solution.py:18
  161.4 0.6 reduce_sum.25
Async XLA Ops:
  0.0 114.1 %copy-start = (bf16[462,512]{1,0:T(8,128)(2,1)S(1)}, bf16[462,512]{1,0:T(8,128)(2,1)}, u32[]{:S(2)}) copy-start(bf16[462,512]{1,0:T(8,128)(2,1)} %param.11) | copy-start | bytes 1419268
  0.0 43.2 %copy-start.4 = (s32[1024]{0:T(1024)S(1)}, s32[1024]{0:T(1024)}, u32[]{:S(2)}) copy-start(s32[1024]{0:T(1024)} %param.7) | copy-start | bytes 12292
  37.9 16.2 %copy-start.1 = (bf16[512,462]{0,1:T(8,128)(2,1)S(1)}, bf16[512,462]{0,1:T(8,128)(2,1)}, u32[]{:S(2)}) copy-start(bf16[512,462]{0,1:T(8,128)(2,1)} %param.9) | copy-start | bytes 1419268
  37.9 16.2 %copy-start.2 = (bf16[512,462]{0,1:T(8,128)(2,1)S(1)}, bf16[512,462]{0,1:T(8,128)(2,1)}, u32[]{:S(2)}) copy-start(bf16[512,462]{0,1:T(8,128)(2,1)} %param.10) | copy-start | bytes 1419268
  37.9 16.2 %copy-start.3 = (f32[512]{0:T(512)S(1)}, f32[512]{0:T(512)}, u32[]{:S(2)}) copy-start(f32[512]{0:T(512)} %param.8) | copy-start | bytes 6148
  38.9 15.2 %all-to-all-start.1 = ((bf16[4,256,512]{2,1,0:T(8,128)(2,1)}), bf16[4,256,512]{2,1,0:T(8,128)(2,1)S(1)}, u32[]{:S(2)}, u32[]{:S(2)}) async-start(bf16[4,256,512]{2,1,0:T(8,128)(2,1)} %broadcast_in_dim.14), calls=%async_computation.1 | async-start | bytes 2097152 | tf_op jit(solution)/shard_map/all_to_all | solution.py:18
  55.4 4.6 %collective-permute-start = (bf16[512,1024]{1,0:T(8,128)(2,1)S(1)}, bf16[512,1024]{1,0:T(8,128)(2,1)S(1)}, u32[]{:S(2)}, u32[]{:S(2)}) collective-permute-start(bf16[512,1024]{1,0:T(8,128)(2,1)S(1)} %products_other.1), channel_id=1, source_target_pairs={{0,64},{64,0},{1,65},{65,1},{2,66},{66,2},{3,67},{67,3},{4,68},{68... | collective-permute-start | bytes 3145736 | tf_op jit(solution)/shard_map/ppermute | solution.py:104

commit v3 on v2

--- a/solution.py
+++ b/solution.py
@@ -9,8 +9,10 @@
 from jax.sharding import PartitionSpec as P
 
 WIDTH = 8192
+X, L = 4, 2
 VM = pl.BlockSpec(memory_space=pltpu.VMEM)
 INTERPRET = False
+NEAR = ("l", "x")
 NT = (((1,), (1,)), ((), ()))
 
 
@@ -28,20 +30,21 @@
 
 
 def products_kernel(sizes, other, source_ref, gathered_ref, gain_ref, gate_ref, up_ref, out_ref, pick_ref, weight_ref):
-    ny, nc, nz, nx, share = sizes
+    ny, nc, nh, nl, nx, share = sizes
+
+    def place(n):
+        return (n % nh * nl + n // (nh * nx)) * nx + n // nh % nx
+
     total = gathered_ref.shape[0]
     units, half = gate_ref.shape[0], weight_ref.shape[0]
     block = total // (ny * nc)
     core = lax.axis_index("c")
     wanted = nc - 1 - core if other else core
     row = lax.broadcasted_iota(jnp.int32, (share, total), 1)
-    token = ((row // share % nz) * nx + row // (share * nz)) * share + row % share
+    token = place(row // share) * share + row % share
     for y in range(ny):
         for k in range(block // share):
-            starts = []
-            for c in range(nc):
-                q = (y * nc + c) * block // share + k
-                starts.append((q % nz * nx + q // nz) * share)
+            starts = [place((y * nc + c) * block // share + k) * share for c in range(nc)]
             start = pl.multiple_of(jnp.where(wanted == 0, starts[0], starts[1]), share)
             ids = source_ref[pl.ds(start, share), :]
             at = y * block + k * share
@@ -94,11 +97,11 @@
 
 
 def on_device(tokens, source, gain, gate_weight, up_weight, down_weight):
-    ny, nc, nz, nx = (lax.axis_size(a) for a in ("y", "c", "z", "x"))
+    ny, nc, nh, nl, nx = (lax.axis_size(a) for a in ("y", "c", "h", "l", "x"))
     share, depth = tokens.shape
-    sizes = (ny, nc, nz, nx, share)
+    sizes = (ny, nc, nh, nl, nx, share)
     units = gate_weight.shape[1]
-    gathered = copied_to_all(copied_to_all(tokens, "z"), "x")
+    gathered = copied_to_all(copied_to_all(tokens, "h"), NEAR)
     operands = (source[:, None], gathered, gain[None, :], gate_weight.T, up_weight.T)
     given = products(sizes, True, jnp.bfloat16, *operands)
     taken = lax.ppermute(given, "c", [(0, 1), (1, 0)])
@@ -107,14 +110,15 @@
     pieces = swapped(both.reshape(ny, -1, both.shape[1]), "y")
     hidden = lax.all_gather(activate(pieces, units), ("y", "c"), axis=0, tiled=True)
     mixed = jnp.dot(hidden, down_weight, preferred_element_type=jnp.float32).astype(jnp.bfloat16)
-    mixed = summed(swapped(mixed.reshape(nx, -1, depth), "x"))
-    return summed(swapped(mixed.reshape(nz, share, depth), "z"))
+    mixed = summed(swapped(mixed.reshape(nl * nx, -1, depth), NEAR))
+    return summed(swapped(mixed.reshape(nh, share, depth), "h"))
 
 
 def solution(mesh):
     row, col = mesh.shape["row"], mesh.shape["col"]
-    finer = Mesh(mesh.devices.reshape(row // 2, 2, col // 4, 4), ("y", "c", "z", "x"))
-    rows, cols = ("y", "c"), ("z", "x")
+    shape = (row // 2, 2, col // (L * X), L, X)
+    finer = Mesh(mesh.devices.reshape(shape), ("y", "c", "h", "l", "x"))
+    rows, cols = ("y", "c"), ("h", "l", "x")
     placed = (P(cols, rows), P(), P(rows), P(rows, cols), P(rows, cols), P(cols, rows))
     return jax.shard_map(
         on_device, mesh=finer, in_specs=placed, out_specs=P(cols, rows), check_vma=False

time: 162 us -> 154 us (0.951)
  blocking collectives: 137 us -> 127 us
  waiting for transfers between devices: 12 us -> 14 us
    all_to_all x4, blocking collectives: 118 us -> 108 us  [swapped(): return lax.all_to_all(value, axis, split_axis=0, concat_axis=0, tiled=True)]
    all_to_all x1, waiting for transfers between devices: 10.7 us -> 12.7 us  [swapped(): return lax.all_to_all(value, axis, split_axis=0, concat_axis=0, tiled=True)]
where the time goes in v3:
time: 154 us
  blocking collectives  127 us (82%)
  waiting for transfers between devices  14 us (9%)
  starting transfers between devices  6.22 us (4%)
  Pallas kernels  2.84 us (2%)
  local copies, waits for them, and re-layouts  2.13 us (1%)
    all_to_all x4, blocking collectives, swapped(): return lax.all_to_all(value, axis, split_axis=0, concat_axis=0, tiled=True)  108 us
    all_gather x1, blocking collectives, on_device(): lax.all_gather(activate(pieces, units), ('y', 'c'), axis=0, tiled=True)  18.5 us
    all_to_all x1, waiting for transfers between devices, swapped(): return lax.all_to_all(value, axis, split_axis=0, concat_axis=0, tiled=True)  12.7 us
    all_to_all x1, starting transfers between devices, swapped(): return lax.all_to_all(value, axis, split_axis=0, concat_axis=0, tiled=True)  4.3 us
  transfers between devices with their start and end apart: 2, of which 2 were waited for; matrix products, arithmetic and copies ran while one was open for 0% of the time, Pallas kernels for 1%

profile of v3, /device:TPU:8, one launch (start us, length us, event | category | flops | bytes accessed | tf_op | source)
XLA Modules:
  0.0 154.1 jit_solution(16037295248240481613)
XLA Ops:
  0.0 0.0 copy-start
  0.0 0.0 copy-start.4
  0.0 0.0 copy-start.2
  0.0 0.0 copy-start.1
  0.0 0.0 copy-start.3
  0.0 0.8 broadcast_in_dim.13
  0.9 35.0 %all_to_all.25 = bf16[8,16,512]{2,1,0:T(8,128)(2,1)S(1)} all-to-all(bf16[8,16,512]{2,1,0:T(8,128)(2,1)S(1)} %broadcast_in_dim.13), channel_id=1, replica_groups=mesh['y'=8,'c'=2,'h'=8,'l'=2,'x'=4] {'h'}, dimensions={0} | all-to-all | bytes 262144 | tf_op jit(solution)/shard_map/all_to_all | solution.py:20
  35.9 1.1 broadcast_in_dim.14
  37.0 4.3 %all-to-all-start.1 = ((bf16[8,128,512]{2,1,0:T(8,128)(2,1)}), bf16[8,128,512]{2,1,0:T(8,128)(2,1)S(1)}, u32[]{:S(2)}, u32[]{:S(2)}) async-start(bf16[8,128,512]{2,1,0:T(8,128)(2,1)} %broadcast_in_dim.14), calls=%async_computation.1 | async-start | bytes 2097152 | tf_op jit(solution)/shard_map/all_to_all | solution.py:20
  41.3 0.0 copy-done.4
  41.3 0.2 copy.9.source_ref
  41.5 12.7 %all-to-all-done.1 = bf16[8,128,512]{2,1,0:T(8,128)(2,1)S(1)} async-done(((bf16[8,128,512]{2,1,0:T(8,128)(2,1)}), bf16[8,128,512]{2,1,0:T(8,128)(2,1)S(1)}, u32[]{:S(2)}, u32[]{:S(2)}) %all-to-all-start.1) | async-done | bytes 1048608 | tf_op jit(solution)/shard_map/all_to_all | solution.py:20
  54.2 0.0 copy-done.2
  54.2 0.0 copy-done.1
  54.2 0.0 copy-done.3
  54.2 1.3 products_other.1
  55.5 1.9 %collective-permute-start = (bf16[512,1024]{1,0:T(8,128)(2,1)S(1)}, bf16[512,1024]{1,0:T(8,128)(2,1)S(1)}, u32[]{:S(2)}, u32[]{:S(2)}) collective-permute-start(bf16[512,1024]{1,0:T(8,128)(2,1)S(1)} %products_other.1), channel_id=1, source_target_pairs={{0,64},{64,0},{1,65},{65,1},{2,66},{66,2},{3,67},{67,3},{4,68},{68... | collective-permute-start | bytes 3145736 | tf_op jit(solution)/shard_map/ppermute | solution.py:107
  57.4 1.3 products_own.1
  58.7 1.3 collective-permute-done
  60.0 0.4 add_convert_fusion
  60.4 34.9 %all_to_all.26.pieces_ref = bf16[8,64,1024]{2,1,0:T(8,128)(2,1)S(1)} all-to-all(bf16[8,64,1024]{2,1,0:T(8,128)(2,1)S(1)} %bitcast.19), channel_id=1, replica_groups=mesh['y'=8,'c'=2,'h'=8,'l'=2,'x'=4] {'y'}, dimensions={0} | all-to-all | bytes 2097152 | tf_op jit(solution)/shard_map/all_to_all | solution.py:20
  95.3 0.2 activate.1
  95.6 18.5 %all_gather.3 = bf16[1024,462]{1,0:T(8,128)(2,1)S(1)} all-gather(bf16[64,462]{1,0:T(8,128)(2,1)S(1)} %activate.1), channel_id=1, replica_groups=mesh['y'=8,'c'=2,'h'=8,'l'=2,'x'=4] {'y','c'}, dimensions={0}, use_global_device_ids=true | all-gather | bytes 1005312 | tf_op jit(solution)/shard_map/all_gather | solution.py:111
  114.1 0.0 copy-done
  114.1 0.7 convolution_convert_fusion
  114.8 19.5 %all_to_all.27 = bf16[8,128,512]{2,1,0:T(8,128)(2,1)S(1)} all-to-all(bf16[8,128,512]{2,1,0:T(8,128)(2,1)S(1)} %bitcast.20), channel_id=1, replica_groups=mesh['y'=8,'c'=2,'h'=8,'l'=2,'x'=4] {'l','x'}, dimensions={0} | all-to-all | bytes 2097152 | tf_op jit(solution)/shard_map/all_to_all | solution.py:20
  134.4 0.1 reduce_sum.24
  134.5 18.9 %all_to_all.28 = bf16[8,16,512]{2,1,0:T(8,128)(2,1)S(1)} all-to-all(bf16[8,16,512]{2,1,0:T(8,128)(2,1)S(1)} %bitcast.22), channel_id=1, replica_groups=mesh['y'=8,'c'=2,'h'=8,'l'=2,'x'=4] {'h'}, dimensions={0} | all-to-all | bytes 262144 | tf_op jit(solution)/shard_map/all_to_all | solution.py:20
  153.5 0.6 reduce_sum.25
Async XLA Ops:
  0.0 114.1 %copy-start = (bf16[462,512]{1,0:T(8,128)(2,1)S(1)}, bf16[462,512]{1,0:T(8,128)(2,1)}, u32[]{:S(2)}) copy-start(bf16[462,512]{1,0:T(8,128)(2,1)} %param.11) | copy-start | bytes 1419268
  0.0 41.3 %copy-start.4 = (s32[1024]{0:T(1024)S(1)}, s32[1024]{0:T(1024)}, u32[]{:S(2)}) copy-start(s32[1024]{0:T(1024)} %param.7) | copy-start | bytes 12292
  0.0 54.2 %copy-start.2 = (bf16[512,462]{0,1:T(8,128)(2,1)S(1)}, bf16[512,462]{0,1:T(8,128)(2,1)}, u32[]{:S(2)}) copy-start(bf16[512,462]{0,1:T(8,128)(2,1)} %param.10) | copy-start | bytes 1419268
  0.0 54.2 %copy-start.1 = (bf16[512,462]{0,1:T(8,128)(2,1)S(1)}, bf16[512,462]{0,1:T(8,128)(2,1)}, u32[]{:S(2)}) copy-start(bf16[512,462]{0,1:T(8,128)(2,1)} %param.9) | copy-start | bytes 1419268
  0.0 54.2 %copy-start.3 = (f32[512]{0:T(512)S(1)}, f32[512]{0:T(512)}, u32[]{:S(2)}) copy-start(f32[512]{0:T(512)} %param.8) | copy-start | bytes 6148
  37.0 17.2 %all-to-all-start.1 = ((bf16[8,128,512]{2,1,0:T(8,128)(2,1)}), bf16[8,128,512]{2,1,0:T(8,128)(2,1)S(1)}, u32[]{:S(2)}, u32[]{:S(2)}) async-start(bf16[8,128,512]{2,1,0:T(8,128)(2,1)} %broadcast_in_dim.14), calls=%async_computation.1 | async-start | bytes 2097152 | tf_op jit(solution)/shard_map/all_to_all | solution.py:20
  55.5 4.6 %collective-permute-start = (bf16[512,1024]{1,0:T(8,128)(2,1)S(1)}, bf16[512,1024]{1,0:T(8,128)(2,1)S(1)}, u32[]{:S(2)}, u32[]{:S(2)}) collective-permute-start(bf16[512,1024]{1,0:T(8,128)(2,1)S(1)} %products_other.1), channel_id=1, source_target_pairs={{0,64},{64,0},{1,65},{65,1},{2,66},{66,2},{3,67},{67,3},{4,68},{68... | collective-permute-start | bytes 3145736 | tf_op jit(solution)/shard_map/ppermute | solution.py:107

commit v4 on v3

--- a/solution.py
+++ b/solution.py
@@ -9,7 +9,7 @@
 from jax.sharding import PartitionSpec as P
 
 WIDTH = 8192
-X, L = 4, 2
+X, L, CHUNKS = 4, 2, 2
 VM = pl.BlockSpec(memory_space=pltpu.VMEM)
 INTERPRET = False
 NEAR = ("l", "x")
@@ -37,18 +37,21 @@
 
     total = gathered_ref.shape[0]
     units, half = gate_ref.shape[0], weight_ref.shape[0]
-    block = total // (ny * nc)
+    block = total // (ny * nc * CHUNKS)
+    part = nh // CHUNKS
     core = lax.axis_index("c")
     wanted = nc - 1 - core if other else core
     row = lax.broadcasted_iota(jnp.int32, (share, total), 1)
     token = place(row // share) * share + row % share
-    for y in range(ny):
-        for k in range(block // share):
-            starts = [place((y * nc + c) * block // share + k) * share for c in range(nc)]
-            start = pl.multiple_of(jnp.where(wanted == 0, starts[0], starts[1]), share)
-            ids = source_ref[pl.ds(start, share), :]
-            at = y * block + k * share
-            pick_ref[at : at + share, :] = jnp.where(ids == token, 1.0, 0.0).astype(jnp.bfloat16)
+    for at in range(0, total // nc, share):
+        chunk, y, k = at // (ny * block), at // block % ny, at % block // share
+        starts = []
+        for c in range(nc):
+            n = (y * nc + c) * block // share + k
+            starts.append(place(n // part * nh + chunk * part + n % part) * share)
+        start = pl.multiple_of(jnp.where(wanted == 0, starts[0], starts[1]), share)
+        ids = source_ref[pl.ds(start, share), :]
+        pick_ref[at : at + share, :] = jnp.where(ids == token, 1.0, 0.0).astype(jnp.bfloat16)
     merged = jnp.dot(pick_ref[...], gathered_ref[...], preferred_element_type=jnp.float32)
     squares = jnp.sum(merged * merged, axis=1, keepdims=True)
     weighted = (merged * gain_ref[...]).astype(jnp.bfloat16)
@@ -107,10 +110,14 @@
     taken = lax.ppermute(given, "c", [(0, 1), (1, 0)])
     own = products(sizes, False, jnp.float32, *operands)
     both = (own + taken.astype(jnp.float32)).astype(jnp.bfloat16)
-    pieces = swapped(both.reshape(ny, -1, both.shape[1]), "y")
-    hidden = lax.all_gather(activate(pieces, units), ("y", "c"), axis=0, tiled=True)
-    mixed = jnp.dot(hidden, down_weight, preferred_element_type=jnp.float32).astype(jnp.bfloat16)
-    mixed = summed(swapped(mixed.reshape(nl * nx, -1, depth), NEAR))
+    pieces = both.reshape(CHUNKS, ny, -1, both.shape[1])
+    pieces = [swapped(pieces[k], "y") for k in range(CHUNKS)]
+    sums = []
+    for piece in pieces:
+        hidden = lax.all_gather(activate(piece, units), ("y", "c"), axis=0, tiled=True)
+        mixed = jnp.dot(hidden, down_weight, preferred_element_type=jnp.float32).astype(jnp.bfloat16)
+        sums.append(summed(swapped(mixed.reshape(nl * nx, -1, depth), NEAR)))
+    mixed = jnp.concatenate(sums, axis=0)
     return summed(swapped(mixed.reshape(nh, share, depth), "h"))
 
 

time: 154 us -> 174 us (1.13)
  starting transfers between devices: 6.22 us -> 20.4 us
  waiting for transfers between devices: 14 us -> 23.9 us
  blocking collectives: 127 us -> 119 us
  matrix products: 0.7 us -> 2.46 us
    all_to_all x4 -> x3, blocking collectives: 108 us -> 78.3 us  [swapped(): return lax.all_to_all(value, axis, split_axis=0, concat_axis=0, tiled=True)]
    all_gather x1 -> x2, blocking collectives: 18.5 us -> 41.1 us  [on_device(): lax.all_gather(activate(piece, units), ('y', 'c'), axis=0, tiled=True)]
    all_to_all x1 -> x4, starting transfers between devices: 4.3 us -> 18.5 us  [swapped(): return lax.all_to_all(value, axis, split_axis=0, concat_axis=0, tiled=True)]
    all_to_all x1 -> x4, waiting for transfers between devices: 12.7 us -> 22.5 us  [swapped(): return lax.all_to_all(value, axis, split_axis=0, concat_axis=0, tiled=True)]
    dot_general x1 -> x2, matrix products: 0.7 us -> 2.46 us  [on_device(): jnp.dot(hidden, down_weight, preferred_element_type=jnp.float32)]
  transfers between devices with their start and end apart: 2 -> 5, of which waited for: 2 -> 3; matrix products, arithmetic and copies ran while one was open for 0% -> 2% of each run, Pallas kernels for 1% -> 1%
where the time goes in v4:
time: 174 us; the launch traced here: 173 us
  blocking collectives  119 us (68%)
  waiting for transfers between devices  23.9 us (14%)
  starting transfers between devices  20.4 us (12%)
  local copies, waits for them, and re-layouts  3 us (2%)
  Pallas kernels  2.86 us (2%)
  matrix products  2.46 us (1%)
    all_to_all x3, blocking collectives, swapped(): return lax.all_to_all(value, axis, split_axis=0, concat_axis=0, tiled=True)  78.3 us
    all_gather x2, blocking collectives, on_device(): lax.all_gather(activate(piece, units), ('y', 'c'), axis=0, tiled=True)  41.1 us
    all_to_all x4, waiting for transfers between devices, swapped(): return lax.all_to_all(value, axis, split_axis=0, concat_axis=0, tiled=True)  22.5 us
    all_to_all x4, starting transfers between devices, swapped(): return lax.all_to_all(value, axis, split_axis=0, concat_axis=0, tiled=True)  18.5 us
  transfers between devices with their start and end apart: 5, of which 3 were waited for; matrix products, arithmetic and copies ran while one was open for 2% of the time, Pallas kernels for 1%

profile of v4, /device:TPU:8, one launch (start us, length us, event | category | flops | bytes accessed | tf_op | source)
XLA Modules:
  0.0 173.3 jit_solution(17295384015874975766)
XLA Ops:
  0.0 0.0 copy-start
  0.0 0.0 copy-start.1
  0.0 0.8 broadcast_in_dim.13
  0.9 35.0 %all_to_all.35 = bf16[8,16,512]{2,1,0:T(8,128)(2,1)S(1)} all-to-all(bf16[8,16,512]{2,1,0:T(8,128)(2,1)S(1)} %broadcast_in_dim.13), channel_id=1, replica_groups=mesh['y'=8,'c'=2,'h'=8,'l'=2,'x'=4] {'h'}, dimensions={0} | all-to-all | bytes 262144 | tf_op jit(solution)/shard_map/all_to_all | solution.py:20
  35.9 1.1 broadcast_in_dim.14
  37.0 4.3 %all-to-all-start.1 = ((bf16[8,128,512]{2,1,0:T(8,128)(2,1)}), bf16[8,128,512]{2,1,0:T(8,128)(2,1)S(1)}, u32[]{:S(2)}, u32[]{:S(2)}) async-start(bf16[8,128,512]{2,1,0:T(8,128)(2,1)} %broadcast_in_dim.14), calls=%async_computation.1 | async-start | bytes 2097152 | tf_op jit(solution)/shard_map/all_to_all | solution.py:20
  41.3 0.2 copy.9.source_ref
  41.5 12.7 %all-to-all-done.1 = bf16[8,128,512]{2,1,0:T(8,128)(2,1)S(1)} async-done(((bf16[8,128,512]{2,1,0:T(8,128)(2,1)}), bf16[8,128,512]{2,1,0:T(8,128)(2,1)S(1)}, u32[]{:S(2)}, u32[]{:S(2)}) %all-to-all-start.1) | async-done | bytes 1048608 | tf_op jit(solution)/shard_map/all_to_all | solution.py:20
  54.2 0.0 copy-done.1
  54.2 1.3 products_other.1
  55.5 1.9 %collective-permute-start = (bf16[512,1024]{1,0:T(8,128)(2,1)S(1)}, bf16[512,1024]{1,0:T(8,128)(2,1)S(1)}, u32[]{:S(2)}, u32[]{:S(2)}) collective-permute-start(bf16[512,1024]{1,0:T(8,128)(2,1)S(1)} %products_other.1), channel_id=1, source_target_pairs={{0,64},{64,0},{1,65},{65,1},{2,66},{66,2},{3,67},{67,3},{4,68},{68... | collective-permute-start | bytes 3145736 | tf_op jit(solution)/shard_map/ppermute | solution.py:110
  57.4 1.3 products_own.1
  58.7 1.3 collective-permute-done
  60.0 0.4 add_convert_fusion
  60.4 0.9 fusion
  61.3 23.7 %all_to_all.36.pieces_ref = bf16[8,32,1024]{2,1,0:T(8,128)(2,1)S(1)} all-to-all(bf16[8,32,1024]{2,1,0:T(8,128)(2,1)S(1)} %bitcast.23), channel_id=1, replica_groups=mesh['y'=8,'c'=2,'h'=8,'l'=2,'x'=4] {'y'}, dimensions={0} | all-to-all | bytes 1048576 | tf_op jit(solution)/shard_map/all_to_all | solution.py:20
  85.0 4.9 %all-to-all-start.4 = ((bf16[8,32,1024]{2,1,0:T(8,128)(2,1)}), bf16[8,32,1024]{2,1,0:T(8,128)(2,1)S(1)}, u32[]{:S(2)}, u32[]{:S(2)}) async-start(bf16[8,32,1024]{2,1,0:T(8,128)(2,1)} %bitcast.8), calls=%async_computation.4 | async-start | bytes 1048576 | tf_op jit(solution)/shard_map/all_to_all | solution.py:20
  89.8 0.1 activate.2
  89.9 23.5 %all_gather.6 = bf16[512,462]{1,0:T(8,128)(2,1)S(1)} all-gather(bf16[32,462]{1,0:T(8,128)(2,1)S(1)} %activate.2), channel_id=1, replica_groups=mesh['y'=8,'c'=2,'h'=8,'l'=2,'x'=4] {'y','c'}, dimensions={0}, use_global_device_ids=true | all-gather | bytes 502656 | tf_op jit(solution)/shard_map/all_gather | solution.py:117
  113.5 1.2 convolution_convert_fusion.1
  114.7 0.0 all-to-all-done.4.pieces_ref
  114.7 3.6 %all-to-all-start.3 = ((bf16[8,64,512]{2,1,0:T(8,128)(2,1)}), bf16[8,64,512]{2,1,0:T(8,128)(2,1)S(1)}, u32[]{:S(2)}, u32[]{:S(2)}) async-start(bf16[8,64,512]{2,1,0:T(8,128)(2,1)} %bitcast.7), calls=%async_computation.3 | async-start | bytes 1048576 | tf_op jit(solution)/shard_map/all_to_all | solution.py:20
  118.3 0.1 activate.3
  118.5 17.6 %all_gather.7 = bf16[512,462]{1,0:T(8,128)(2,1)S(1)} all-gather(bf16[32,462]{1,0:T(8,128)(2,1)S(1)} %activate.3), channel_id=1, replica_groups=mesh['y'=8,'c'=2,'h'=8,'l'=2,'x'=4] {'y','c'}, dimensions={0}, use_global_device_ids=true | all-gather | bytes 502656 | tf_op jit(solution)/shard_map/all_gather | solution.py:117
  136.1 1.2 convolution_convert_fusion
  137.3 0.0 all-to-all-done.3
  137.3 5.7 %all-to-all-start.5 = ((bf16[8,64,512]{2,1,0:T(8,128)(2,1)}), bf16[8,64,512]{2,1,0:T(8,128)(2,1)S(1)}, u32[]{:S(2)}, u32[]{:S(2)}) async-start(bf16[8,64,512]{2,1,0:T(8,128)(2,1)} %bitcast.9), calls=%async_computation.5 | async-start | bytes 1048576 | tf_op jit(solution)/shard_map/all_to_all | solution.py:20
  143.0 0.1 reduce_sum.36
  143.1 9.9 %all-to-all-done.5 = bf16[8,64,512]{2,1,0:T(8,128)(2,1)S(1)} async-done(((bf16[8,64,512]{2,1,0:T(8,128)(2,1)}), bf16[8,64,512]{2,1,0:T(8,128)(2,1)S(1)}, u32[]{:S(2)}, u32[]{:S(2)}) %all-to-all-start.5) | async-done | bytes 524320 | tf_op jit(solution)/shard_map/all_to_all | solution.py:20
  152.9 0.1 reduce_sum.37
  153.0 19.6 %all_to_all.37 = bf16[8,16,512]{2,1,0:T(8,128)(2,1)S(1)} all-to-all(bf16[8,16,512]{2,1,0:T(8,128)(2,1)S(1)} %bitcast.25), channel_id=1, replica_groups=mesh['y'=8,'c'=2,'h'=8,'l'=2,'x'=4] {'h'}, dimensions={0} | all-to-all | bytes 262144 | tf_op jit(solution)/shard_map/all_to_all | solution.py:20
  172.7 0.6 reduce_sum.38
  (8 shorter events, 0.0 us)
Async XLA Ops:
  0.0 113.5 %copy-start = (bf16[462,512]{1,0:T(8,128)(2,1)S(1)}, bf16[462,512]{1,0:T(8,128)(2,1)}, u32[]{:S(2)}) copy-start(bf16[462,512]{1,0:T(8,128)(2,1)} %param.11) | copy-start | bytes 1419268
  0.0 41.3 %copy-start.4 = (s32[1024]{0:T(1024)S(1)}, s32[1024]{0:T(1024)}, u32[]{:S(2)}) copy-start(s32[1024]{0:T(1024)} %param.7) | copy-start | bytes 12292
  0.0 54.2 %copy-start.2 = (bf16[512,462]{0,1:T(8,128)(2,1)S(1)}, bf16[512,462]{0,1:T(8,128)(2,1)}, u32[]{:S(2)}) copy-start(bf16[512,462]{0,1:T(8,128)(2,1)} %param.10) | copy-start | bytes 1419268
  0.0 54.2 %copy-start.1 = (bf16[512,462]{0,1:T(8,128)(2,1)S(1)}, bf16[512,462]{0,1:T(8,128)(2,1)}, u32[]{:S(2)}) copy-start(bf16[512,462]{0,1:T(8,128)(2,1)} %param.9) | copy-start | bytes 1419268
  0.0 54.2 %copy-start.3 = (f32[512]{0:T(512)S(1)}, f32[512]{0:T(512)}, u32[]{:S(2)}) copy-start(f32[512]{0:T(512)} %param.8) | copy-start | bytes 6148
  37.0 17.2 %all-to-all-start.1 = ((bf16[8,128,512]{2,1,0:T(8,128)(2,1)}), bf16[8,128,512]{2,1,0:T(8,128)(2,1)S(1)}, u32[]{:S(2)}, u32[]{:S(2)}) async-start(bf16[8,128,512]{2,1,0:T(8,128)(2,1)} %broadcast_in_dim.14), calls=%async_computation.1 | async-start | bytes 2097152 | tf_op jit(solution)/shard_map/all_to_all | solution.py:20
  55.5 4.6 %collective-permute-start = (bf16[512,1024]{1,0:T(8,128)(2,1)S(1)}, bf16[512,1024]{1,0:T(8,128)(2,1)S(1)}, u32[]{:S(2)}, u32[]{:S(2)}) collective-permute-start(bf16[512,1024]{1,0:T(8,128)(2,1)S(1)} %products_other.1), channel_id=1, source_target_pairs={{0,64},{64,0},{1,65},{65,1},{2,66},{66,2},{3,67},{67,3},{4,68},{68... | collective-permute-start | bytes 3145736 | tf_op jit(solution)/shard_map/ppermute | solution.py:110
  85.0 29.7 %all-to-all-start.4 = ((bf16[8,32,1024]{2,1,0:T(8,128)(2,1)}), bf16[8,32,1024]{2,1,0:T(8,128)(2,1)S(1)}, u32[]{:S(2)}, u32[]{:S(2)}) async-start(bf16[8,32,1024]{2,1,0:T(8,128)(2,1)} %bitcast.8), calls=%async_computation.4 | async-start | bytes 1048576 | tf_op jit(solution)/shard_map/all_to_all | solution.py:20
  114.7 22.6 %all-to-all-start.3 = ((bf16[8,64,512]{2,1,0:T(8,128)(2,1)}), bf16[8,64,512]{2,1,0:T(8,128)(2,1)S(1)}, u32[]{:S(2)}, u32[]{:S(2)}) async-start(bf16[8,64,512]{2,1,0:T(8,128)(2,1)} %bitcast.7), calls=%async_computation.3 | async-start | bytes 1048576 | tf_op jit(solution)/shard_map/all_to_all | solution.py:20
  137.3 15.6 %all-to-all-start.5 = ((bf16[8,64,512]{2,1,0:T(8,128)(2,1)}), bf16[8,64,512]{2,1,0:T(8,128)(2,1)S(1)}, u32[]{:S(2)}, u32[]{:S(2)}) async-start(bf16[8,64,512]{2,1,0:T(8,128)(2,1)} %bitcast.9), calls=%async_computation.5 | async-start | bytes 1048576 | tf_op jit(solution)/shard_map/all_to_all | solution.py:20

commit v5 on v3

--- a/solution.py
+++ b/solution.py
@@ -10,6 +10,7 @@
 
 WIDTH = 8192
 X, L = 4, 2
+LANES, FOLD = 128, 4
 VM = pl.BlockSpec(memory_space=pltpu.VMEM)
 INTERPRET = False
 NEAR = ("l", "x")
@@ -55,43 +56,77 @@
     weight_ref[units:, :] = jnp.zeros((half - units, weight_ref.shape[1]), jnp.bfloat16)
     weight_ref[:units, :] = gate_ref[...]
     gate = lax.dot_general(weighted, weight_ref[...], NT, preferred_element_type=jnp.float32)
-    lane = lax.broadcasted_iota(jnp.int32, gate.shape, 1)
-    out_ref[:, :half] = jnp.where(lane == units, squares, gate).astype(out_ref.dtype)
     weight_ref[:units, :] = up_ref[...]
     up = lax.dot_general(weighted, weight_ref[...], NT, preferred_element_type=jnp.float32)
-    out_ref[:, half:] = up.astype(out_ref.dtype)
+    full, tail = units // LANES, units % LANES
+    over = 2 * tail - LANES
+    rolled = pltpu.roll(up[:, full * LANES :], tail, 1)
+    lane = lax.broadcasted_iota(jnp.int32, rolled.shape, 1)
+    shared = jnp.where(lane < tail, gate[:, full * LANES :], rolled)
+    rest = jnp.where(lane < over, rolled, jnp.where(lane == over, squares, 0.0))
+    tiles = [v[:, t * LANES : (t + 1) * LANES] for v in (gate, up) for t in range(full)] + [shared]
+    quarter = block // FOLD
+    for y in range(ny):
+        for t, tile in enumerate(tiles):
+            out_ref[y, t * block : (t + 1) * block, :] = tile[y * block : (y + 1) * block].astype(out_ref.dtype)
+        folded = rest[y * block : y * block + quarter]
+        for k in range(1, FOLD):
+            at = y * block + k * quarter
+            folded += pltpu.roll(rest[at : at + quarter], k * LANES // FOLD, 1)
+        out_ref[y, len(tiles) * block :, :] = folded.astype(out_ref.dtype)
 
 
 def products(sizes, other, kind, source, gathered, gain, gate_weight, up_weight):
     units, depth = gate_weight.shape
-    half = -(-(units + 1) // 128) * 128
-    kept = gathered.shape[0] // sizes[1]
+    full, tail = units // LANES, units % LANES
+    assert LANES <= 2 * tail < LANES + LANES // FOLD
+    ny, nc = sizes[:2]
+    kept = gathered.shape[0] // nc
+    rows = kept // ny * (2 * full + 1) + kept // ny // FOLD
     return pl.pallas_call(
         functools.partial(products_kernel, sizes, other),
-        out_shape=jax.ShapeDtypeStruct((kept, 2 * half), kind),
+        out_shape=jax.ShapeDtypeStruct((ny, rows, LANES), kind),
+        in_specs=[VM] * 5,
+        out_specs=VM,
         scratch_shapes=[
             pltpu.VMEM((kept, gathered.shape[0]), jnp.bfloat16),
-            pltpu.VMEM((half, depth), jnp.bfloat16),
+            pltpu.VMEM(((full + 1) * LANES, depth), jnp.bfloat16),
         ],
-        interpret=INTERPRET, compiler_params=pltpu.CompilerParams(vmem_limit_bytes=16 << 20), in_specs=[VM] * 5, out_specs=VM,
+        interpret=INTERPRET,
+        compiler_params=pltpu.CompilerParams(vmem_limit_bytes=16 << 20),
         name="products_other" if other else "products_own",
     )(source, gathered, gain, gate_weight, up_weight)
 
 
 def activate_kernel(units, pieces_ref, out_ref):
     total = jnp.sum(pieces_ref[...].astype(jnp.float32), axis=0)
-    half = total.shape[1] // 2
-    gate, up = total[:, :half], total[:, half:]
-    scale = lax.rsqrt(gate[:, units : units + 1] / WIDTH + 1e-6)
-    gate, up = scale * gate[:, :units], scale * up[:, :units]
-    out_ref[...] = (gate / (1.0 + jnp.exp(-gate)) * up).astype(jnp.bfloat16)
+    full, tail = units // LANES, units % LANES
+    block = out_ref.shape[0]
+    tiles = [total[t * block : (t + 1) * block] for t in range(2 * full + 1)]
+    folded = total[(2 * full + 1) * block :]
+    parts = [folded] + [pltpu.roll(folded, LANES - k * LANES // FOLD, 1) for k in range(1, FOLD)]
+    rest = jnp.concatenate(parts, axis=0)
+    over = 2 * tail - LANES
+    scale = lax.rsqrt(rest[:, over : over + 1] / WIDTH + 1e-6)
+    shared = tiles[2 * full]
+    lane = lax.broadcasted_iota(jnp.int32, shared.shape, 1)
+    last = pltpu.roll(jnp.where(lane < tail, rest, shared), LANES - tail, 1)
+    gates, ups = tiles[:full] + [shared], tiles[full : 2 * full] + [last]
+    for t in range(full + 1):
+        gate, up = scale * gates[t], scale * ups[t]
+        value = (gate / (1.0 + jnp.exp(-gate)) * up).astype(jnp.bfloat16)
+        width = LANES if t < full else tail
+        out_ref[:, t * LANES : t * LANES + width] = value[:, :width]
 
 
-def activate(pieces, units):
+def activate(pieces, units, share):
     return pl.pallas_call(
         functools.partial(activate_kernel, units),
-        out_shape=jax.ShapeDtypeStruct((pieces.shape[1], units), jnp.bfloat16),
-        interpret=INTERPRET, compiler_params=pltpu.CompilerParams(vmem_limit_bytes=16 << 20), in_specs=[VM], out_specs=VM,
+        out_shape=jax.ShapeDtypeStruct((share, units), jnp.bfloat16),
+        in_specs=[VM],
+        out_specs=VM,
+        interpret=INTERPRET,
+        compiler_params=pltpu.CompilerParams(vmem_limit_bytes=16 << 20),
         name="activate",
     )(pieces)
 
@@ -107,8 +142,8 @@
     taken = lax.ppermute(given, "c", [(0, 1), (1, 0)])
     own = products(sizes, False, jnp.float32, *operands)
     both = (own + taken.astype(jnp.float32)).astype(jnp.bfloat16)
-    pieces = swapped(both.reshape(ny, -1, both.shape[1]), "y")
-    hidden = lax.all_gather(activate(pieces, units), ("y", "c"), axis=0, tiled=True)
+    pieces = swapped(both, "y")
+    hidden = lax.all_gather(activate(pieces, units, gathered.shape[0] // (ny * nc)), ("y", "c"), axis=0, tiled=True)
     mixed = jnp.dot(hidden, down_weight, preferred_element_type=jnp.float32).astype(jnp.bfloat16)
     mixed = summed(swapped(mixed.reshape(nl * nx, -1, depth), NEAR))
     return summed(swapped(mixed.reshape(nh, share, depth), "h"))

time: 154 us -> 152 us (0.987)
  blocking collectives: 127 us -> 125 us
    all_to_all x4, blocking collectives: 108 us -> 106 us  [swapped(): return lax.all_to_all(value, axis, split_axis=0, concat_axis=0, tiled=True)]
where the time goes in v5:
time: 152 us
  blocking collectives  125 us (82%)
  waiting for transfers between devices  13.7 us (9%)
  starting transfers between devices  6.22 us (4%)
  Pallas kernels  3.1 us (2%)
  local copies, waits for them, and re-layouts  2.1 us (1%)
    all_to_all x4, blocking collectives, swapped(): return lax.all_to_all(value, axis, split_axis=0, concat_axis=0, tiled=True)  106 us
    all_gather x1, blocking collectives, on_device(): lax.all_gather(activate(pieces, units, gathered.shape[0] // (ny * nc)), (...  18.5 us
    all_to_all x1, waiting for transfers between devices, swapped(): return lax.all_to_all(value, axis, split_axis=0, concat_axis=0, tiled=True)  12.7 us
    all_to_all x1, starting transfers between devices, swapped(): return lax.all_to_all(value, axis, split_axis=0, concat_axis=0, tiled=True)  4.3 us
  transfers between devices with their start and end apart: 2, of which 2 were waited for; matrix products, arithmetic and copies ran while one was open for 0% of the time, Pallas kernels for 1%

profile of v5, /device:TPU:8, one launch (start us, length us, event | category | flops | bytes accessed | tf_op | source)
XLA Modules:
  0.0 151.7 jit_solution(6579721352848297979)
XLA Ops:
  0.0 0.0 copy-start
  0.0 0.0 copy-start.4
  0.0 0.8 broadcast_in_dim.13
  0.8 35.0 %all_to_all.25 = bf16[8,16,512]{2,1,0:T(8,128)(2,1)S(1)} all-to-all(bf16[8,16,512]{2,1,0:T(8,128)(2,1)S(1)} %broadcast_in_dim.13), channel_id=1, replica_groups=mesh['y'=8,'c'=2,'h'=8,'l'=2,'x'=4] {'h'}, dimensions={0} | all-to-all | bytes 262144 | tf_op jit(solution)/shard_map/all_to_all | solution.py:21
  35.8 0.0 copy-start.1
  35.8 0.0 copy-start.2
  35.8 0.0 copy-start.3
  35.8 1.1 broadcast_in_dim.14
  36.9 4.3 %all-to-all-start.1 = ((bf16[8,128,512]{2,1,0:T(8,128)(2,1)}), bf16[8,128,512]{2,1,0:T(8,128)(2,1)S(1)}, u32[]{:S(2)}, u32[]{:S(2)}) async-start(bf16[8,128,512]{2,1,0:T(8,128)(2,1)} %broadcast_in_dim.14), calls=%async_computation.1 | async-start | bytes 2097152 | tf_op jit(solution)/shard_map/all_to_all | solution.py:21
  41.2 0.0 copy-done.4
  41.2 0.2 copy.9.source_ref
  41.4 12.7 %all-to-all-done.1 = bf16[8,128,512]{2,1,0:T(8,128)(2,1)S(1)} async-done(((bf16[8,128,512]{2,1,0:T(8,128)(2,1)}), bf16[8,128,512]{2,1,0:T(8,128)(2,1)S(1)}, u32[]{:S(2)}, u32[]{:S(2)}) %all-to-all-start.1) | async-done | bytes 1048608 | tf_op jit(solution)/shard_map/all_to_all | solution.py:21
  54.1 0.0 copy-done.1
  54.1 0.0 copy-done.2
  54.1 0.0 copy-done.3
  54.1 1.4 products_other.1
  55.6 1.9 %collective-permute-start = (bf16[8,464,128]{2,1,0:T(8,128)(2,1)S(1)}, bf16[8,464,128]{2,1,0:T(8,128)(2,1)S(1)}, u32[]{:S(2)}, u32[]{:S(2)}) collective-permute-start(bf16[8,464,128]{2,1,0:T(8,128)(2,1)S(1)} %products_other.1), channel_id=1, source_target_pairs={{0,64},{64,0},{1,65},{65,1},{2,66},{66,2},{3,67},{67,3},{4,68},{68... | collective-permute-start | bytes 2850824 | tf_op jit(solution)/shard_map/ppermute | solution.py:142
  57.5 1.4 products_own.1
  58.9 1.0 collective-permute-done
  60.0 0.2 add_convert_fusion
  60.2 32.8 %all_to_all.26.pieces_ref = bf16[8,464,128]{2,1,0:T(8,128)(2,1)S(1)} all-to-all(bf16[8,464,128]{2,1,0:T(8,128)(2,1)S(1)} %add_convert_fusion), channel_id=1, replica_groups=mesh['y'=8,'c'=2,'h'=8,'l'=2,'x'=4] {'y'}, dimensions={0} | all-to-all | bytes 1900544 | tf_op jit(solution)/shard_map/all_to_all | solution.py:21
  93.0 0.2 activate.1
  93.2 18.5 %all_gather.3 = bf16[1024,462]{1,0:T(8,128)(2,1)S(1)} all-gather(bf16[64,462]{1,0:T(8,128)(2,1)S(1)} %activate.1), channel_id=1, replica_groups=mesh['y'=8,'c'=2,'h'=8,'l'=2,'x'=4] {'y','c'}, dimensions={0}, use_global_device_ids=true | all-gather | bytes 1005312 | tf_op jit(solution)/shard_map/all_gather | solution.py:146
  111.7 0.0 copy-done
  111.7 0.7 convolution_convert_fusion
  112.4 19.5 %all_to_all.27 = bf16[8,128,512]{2,1,0:T(8,128)(2,1)S(1)} all-to-all(bf16[8,128,512]{2,1,0:T(8,128)(2,1)S(1)} %bitcast.18), channel_id=1, replica_groups=mesh['y'=8,'c'=2,'h'=8,'l'=2,'x'=4] {'l','x'}, dimensions={0} | all-to-all | bytes 2097152 | tf_op jit(solution)/shard_map/all_to_all | solution.py:21
  132.0 0.1 reduce_sum.24
  132.1 18.9 %all_to_all.28 = bf16[8,16,512]{2,1,0:T(8,128)(2,1)S(1)} all-to-all(bf16[8,16,512]{2,1,0:T(8,128)(2,1)S(1)} %bitcast.20), channel_id=1, replica_groups=mesh['y'=8,'c'=2,'h'=8,'l'=2,'x'=4] {'h'}, dimensions={0} | all-to-all | bytes 262144 | tf_op jit(solution)/shard_map/all_to_all | solution.py:21
  151.1 0.6 reduce_sum.25
Async XLA Ops:
  0.0 111.7 %copy-start = (bf16[462,512]{1,0:T(8,128)(2,1)S(1)}, bf16[462,512]{1,0:T(8,128)(2,1)}, u32[]{:S(2)}) copy-start(bf16[462,512]{1,0:T(8,128)(2,1)} %param.11) | copy-start | bytes 1419268
  0.0 41.2 %copy-start.4 = (s32[1024]{0:T(1024)S(1)}, s32[1024]{0:T(1024)}, u32[]{:S(2)}) copy-start(s32[1024]{0:T(1024)} %param.7) | copy-start | bytes 12292
  35.8 18.3 %copy-start.1 = (bf16[512,462]{0,1:T(8,128)(2,1)S(1)}, bf16[512,462]{0,1:T(8,128)(2,1)}, u32[]{:S(2)}) copy-start(bf16[512,462]{0,1:T(8,128)(2,1)} %param.9) | copy-start | bytes 1419268
  35.8 18.3 %copy-start.2 = (bf16[512,462]{0,1:T(8,128)(2,1)S(1)}, bf16[512,462]{0,1:T(8,128)(2,1)}, u32[]{:S(2)}) copy-start(bf16[512,462]{0,1:T(8,128)(2,1)} %param.10) | copy-start | bytes 1419268
  35.8 18.3 %copy-start.3 = (f32[512]{0:T(512)S(1)}, f32[512]{0:T(512)}, u32[]{:S(2)}) copy-start(f32[512]{0:T(512)} %param.8) | copy-start | bytes 6148
  36.9 17.2 %all-to-all-start.1 = ((bf16[8,128,512]{2,1,0:T(8,128)(2,1)}), bf16[8,128,512]{2,1,0:T(8,128)(2,1)S(1)}, u32[]{:S(2)}, u32[]{:S(2)}) async-start(bf16[8,128,512]{2,1,0:T(8,128)(2,1)} %broadcast_in_dim.14), calls=%async_computation.1 | async-start | bytes 2097152 | tf_op jit(solution)/shard_map/all_to_all | solution.py:21
  55.6 4.4 %collective-permute-start = (bf16[8,464,128]{2,1,0:T(8,128)(2,1)S(1)}, bf16[8,464,128]{2,1,0:T(8,128)(2,1)S(1)}, u32[]{:S(2)}, u32[]{:S(2)}) collective-permute-start(bf16[8,464,128]{2,1,0:T(8,128)(2,1)S(1)} %products_other.1), channel_id=1, source_target_pairs={{0,64},{64,0},{1,65},{65,1},{2,66},{66,2},{3,67},{67,3},{4,68},{68... | collective-permute-start | bytes 2850824 | tf_op jit(solution)/shard_map/ppermute | solution.py:142

commit v6 on v5

--- a/solution.py
+++ b/solution.py
@@ -30,34 +30,72 @@
     return jnp.sum(pieces.astype(jnp.float32), axis=0).astype(jnp.bfloat16)
 
 
-def products_kernel(sizes, other, source_ref, gathered_ref, gain_ref, gate_ref, up_ref, out_ref, pick_ref, weight_ref):
+def pick_kernel(sizes, source_ref, out_ref):
     ny, nc, nh, nl, nx, share = sizes
+    total, part = out_ref.shape[0], share // nc
 
-    def place(n):
-        return (n % nh * nl + n // (nh * nx)) * nx + n // nh % nx
+    def place(h, near):
+        return ((h * nl + near // nx) * nx + near % nx) * share
 
-    total = gathered_ref.shape[0]
-    units, half = gate_ref.shape[0], weight_ref.shape[0]
+    row = lax.broadcasted_iota(jnp.int32, (share, total), 1)
     block = total // (ny * nc)
+    kept = row // (nc * block) * block + row % block
+    token = place(kept // part % nh, kept // (part * nh)) + row // block % nc * part + kept % part
+    for at in range(0, total, share):
+        n = at // share
+        start = place(n % nh, n // nh)
+        ids = source_ref[start : start + share, :]
+        out_ref[at : at + share, :] = jnp.where(ids == token, 1.0, 0.0).astype(jnp.bfloat16)
+
+
+def pick_rows(sizes, source):
+    total = source.shape[0]
+    return pl.pallas_call(
+        functools.partial(pick_kernel, sizes),
+        out_shape=jax.ShapeDtypeStruct((total, total), jnp.bfloat16),
+        in_specs=[VM],
+        out_specs=VM,
+        interpret=INTERPRET,
+        compiler_params=pltpu.CompilerParams(vmem_limit_bytes=16 << 20),
+        name="pick_rows",
+    )(source[:, None])
+
+
+def mixed_kernel(pick_ref, hidden_ref, down_ref, out_ref):
+    chosen = jnp.dot(pick_ref[...], hidden_ref[...], preferred_element_type=jnp.float32)
+    chosen = chosen.astype(jnp.bfloat16)
+    out = jnp.dot(chosen, down_ref[...], preferred_element_type=jnp.float32)
+    out_ref[...] = out.astype(jnp.bfloat16)
+
+
+def mixed_rows(pick, hidden, down_weight):
+    return pl.pallas_call(
+        mixed_kernel,
+        out_shape=jax.ShapeDtypeStruct((pick.shape[0], down_weight.shape[1]), jnp.bfloat16),
+        in_specs=[VM] * 3,
+        out_specs=VM,
+        interpret=INTERPRET,
+        compiler_params=pltpu.CompilerParams(vmem_limit_bytes=24 << 20),
+        name="mixed_rows",
+    )(pick, hidden, down_weight)
+
+
+def products_kernel(gathered_ref, *refs):
+    sides, (out_ref, weight_ref) = (refs[:3], refs[3:6]), refs[6:]
+    ny, depth, units = out_ref.shape[0], gathered_ref.shape[3], refs[1].shape[0]
+    kept = gathered_ref.shape[0] * gathered_ref.shape[2]
+    block = kept // ny
+    weight_ref[units:, :] = jnp.zeros((weight_ref.shape[0] - units, depth), jnp.bfloat16)
     core = lax.axis_index("c")
-    wanted = nc - 1 - core if other else core
-    row = lax.broadcasted_iota(jnp.int32, (share, total), 1)
-    token = place(row // share) * share + row % share
-    for y in range(ny):
-        for k in range(block // share):
-            starts = [place((y * nc + c) * block // share + k) * share for c in range(nc)]
-            start = pl.multiple_of(jnp.where(wanted == 0, starts[0], starts[1]), share)
-            ids = source_ref[pl.ds(start, share), :]
-            at = y * block + k * share
-            pick_ref[at : at + share, :] = jnp.where(ids == token, 1.0, 0.0).astype(jnp.bfloat16)
-    merged = jnp.dot(pick_ref[...], gathered_ref[...], preferred_element_type=jnp.float32)
-    squares = jnp.sum(merged * merged, axis=1, keepdims=True)
-    weighted = (merged * gain_ref[...]).astype(jnp.bfloat16)
-    weight_ref[units:, :] = jnp.zeros((half - units, weight_ref.shape[1]), jnp.bfloat16)
-    weight_ref[:units, :] = gate_ref[...]
-    gate = lax.dot_general(weighted, weight_ref[...], NT, preferred_element_type=jnp.float32)
-    weight_ref[:units, :] = up_ref[...]
-    up = lax.dot_general(weighted, weight_ref[...], NT, preferred_element_type=jnp.float32)
+    squares, gate, up = 0.0, 0.0, 0.0
+    for side, (gain_ref, gate_ref, up_ref) in zip((core, 1 - core), sides):
+        merged = gathered_ref[:, pl.ds(side, 1)].astype(jnp.float32).reshape(kept, depth)
+        squares += jnp.sum(merged * merged, axis=1, keepdims=True)
+        weighted = (merged * gain_ref[...]).astype(jnp.bfloat16)
+        weight_ref[:units, :] = gate_ref[...]
+        gate += lax.dot_general(weighted, weight_ref[...], NT, preferred_element_type=jnp.float32)
+        weight_ref[:units, :] = up_ref[...]
+        up += lax.dot_general(weighted, weight_ref[...], NT, preferred_element_type=jnp.float32)
     full, tail = units // LANES, units % LANES
     over = 2 * tail - LANES
     rolled = pltpu.roll(up[:, full * LANES :], tail, 1)
@@ -76,26 +114,22 @@
         out_ref[y, len(tiles) * block :, :] = folded.astype(out_ref.dtype)
 
 
-def products(sizes, other, kind, source, gathered, gain, gate_weight, up_weight):
-    units, depth = gate_weight.shape
+def products(ny, gathered, *sides):
+    units, depth = sides[1].shape
     full, tail = units // LANES, units % LANES
     assert LANES <= 2 * tail < LANES + LANES // FOLD
-    ny, nc = sizes[:2]
-    kept = gathered.shape[0] // nc
-    rows = kept // ny * (2 * full + 1) + kept // ny // FOLD
+    block = gathered.shape[0] * gathered.shape[2] // ny
+    rows = block * (2 * full + 1) + block // FOLD
     return pl.pallas_call(
-        functools.partial(products_kernel, sizes, other),
-        out_shape=jax.ShapeDtypeStruct((ny, rows, LANES), kind),
-        in_specs=[VM] * 5,
+        products_kernel,
+        out_shape=jax.ShapeDtypeStruct((ny, rows, LANES), jnp.bfloat16),
+        in_specs=[VM] * 7,
         out_specs=VM,
-        scratch_shapes=[
-            pltpu.VMEM((kept, gathered.shape[0]), jnp.bfloat16),
-            pltpu.VMEM(((full + 1) * LANES, depth), jnp.bfloat16),
-        ],
+        scratch_shapes=[pltpu.VMEM(((full + 1) * LANES, depth), jnp.bfloat16)],
         interpret=INTERPRET,
-        compiler_params=pltpu.CompilerParams(vmem_limit_bytes=16 << 20),
-        name="products_other" if other else "products_own",
-    )(source, gathered, gain, gate_weight, up_weight)
+        compiler_params=pltpu.CompilerParams(vmem_limit_bytes=24 << 20),
+        name="products",
+    )(gathered, *sides)
 
 
 def activate_kernel(units, pieces_ref, out_ref):
@@ -134,17 +168,17 @@
 def on_device(tokens, source, gain, gate_weight, up_weight, down_weight):
     ny, nc, nh, nl, nx = (lax.axis_size(a) for a in ("y", "c", "h", "l", "x"))
     share, depth = tokens.shape
+    units, part = gate_weight.shape[1], share // nc
     sizes = (ny, nc, nh, nl, nx, share)
-    units = gate_weight.shape[1]
-    gathered = copied_to_all(copied_to_all(tokens, "h"), NEAR)
-    operands = (source[:, None], gathered, gain[None, :], gate_weight.T, up_weight.T)
-    given = products(sizes, True, jnp.bfloat16, *operands)
-    taken = lax.ppermute(given, "c", [(0, 1), (1, 0)])
-    own = products(sizes, False, jnp.float32, *operands)
-    both = (own + taken.astype(jnp.float32)).astype(jnp.bfloat16)
-    pieces = swapped(both, "y")
-    hidden = lax.all_gather(activate(pieces, units, gathered.shape[0] // (ny * nc)), ("y", "c"), axis=0, tiled=True)
-    mixed = jnp.dot(hidden, down_weight, preferred_element_type=jnp.float32).astype(jnp.bfloat16)
+    halves = jnp.broadcast_to(tokens.reshape(nc, 1, part, depth), (nc, nh, part, depth))
+    halves = swapped(halves.reshape(nc * nh, part, depth), ("c", "h")).reshape(-1, depth)
+    gathered = copied_to_all(halves, NEAR).reshape(nl * nx, nc, nh * part, depth)
+    own = (gain[None, :], gate_weight.T, up_weight.T)
+    other = [lax.ppermute(v, "c", [(0, 1), (1, 0)]) for v in own]
+    pieces = swapped(products(ny, gathered, *own, *other), "y")
+    hidden = activate(pieces, units, nl * nx * nh * part // ny)
+    hidden = lax.all_gather(hidden, ("y", "c"), axis=0, tiled=True)
+    mixed = mixed_rows(pick_rows(sizes, source), hidden, down_weight)
     mixed = summed(swapped(mixed.reshape(nl * nx, -1, depth), NEAR))
     return summed(swapped(mixed.reshape(nh, share, depth), "h"))
 

time: 152 us -> 151 us (level)
  blocking collectives: 125 us -> 92.7 us
  waiting for transfers between devices: 13.7 us -> 28.5 us
  starting transfers between devices: 6.22 us -> 19.3 us
  local copies, waits for them, and re-layouts: 2.1 us -> 3.96 us
  Pallas kernels: 3.1 us -> 4.82 us
    all_to_all x4 -> x3, blocking collectives: 106 us -> 74.2 us  [swapped(): return lax.all_to_all(value, axis, split_axis=0, concat_axis=0, tiled=True)]
    all_to_all x1 -> x2, waiting for transfers between devices: 12.7 us -> 27.3 us  [swapped(): return lax.all_to_all(value, axis, split_axis=0, concat_axis=0, tiled=True)]
    all_to_all x1 -> x2, starting transfers between devices: 4.3 us -> 13 us  [swapped(): return lax.all_to_all(value, axis, split_axis=0, concat_axis=0, tiled=True)]
    ppermute x1 -> x3, starting transfers between devices: 1.92 us -> 6.25 us  [on_device(): other = [lax.ppermute(v, 'c', [(0, 1), (1, 0)]) for v in own]]
    pallas_call x2 -> x3, Pallas kernels: 2.89 us -> 4.61 us  [the longest x1 2.4 us: products(): pl.pallas_call(products_kernel, out_shape=jax.ShapeDtypeStruct((ny, rows,...]
    broadcast_in_dim x1 -> x2, local copies, waits for them, and re-layouts: 0.22 us -> 1.85 us  [the longest x1 1.04 us: pick_rows(): source[:, None]]
  transfers between devices with their start and end apart: 2 -> 5, of which waited for: 2 -> 3; matrix products, arithmetic and copies ran while one was open for 0% -> 1% of each run, Pallas kernels for 1% -> 0%
where the time goes in v6:
time: 151 us; the launch traced here: 150 us
  blocking collectives  92.7 us (61%)
  waiting for transfers between devices  28.5 us (19%)
  starting transfers between devices  19.3 us (13%)
  Pallas kernels  4.82 us (3%)
  local copies, waits for them, and re-layouts  3.96 us (3%)
    all_to_all x3, blocking collectives, swapped(): return lax.all_to_all(value, axis, split_axis=0, concat_axis=0, tiled=True)  74.2 us
    all_to_all x2, waiting for transfers between devices, swapped(): return lax.all_to_all(value, axis, split_axis=0, concat_axis=0, tiled=True)  27.3 us
    all_gather x1, blocking collectives, on_device(): hidden = lax.all_gather(hidden, ('y', 'c'), axis=0, tiled=True)  18.5 us
    all_to_all x2, starting transfers between devices, swapped(): return lax.all_to_all(value, axis, split_axis=0, concat_axis=0, tiled=True)  13 us
    ppermute x3, starting transfers between devices, on_device(): other = [lax.ppermute(v, 'c', [(0, 1), (1, 0)]) for v in own]  6.25 us
  transfers between devices with their start and end apart: 5, of which 3 were waited for; matrix products, arithmetic and copies ran while one was open for 1% of the time, Pallas kernels for 0%

profile of v6, /device:TPU:8, one launch (start us, length us, event | category | flops | bytes accessed | tf_op | source)
XLA Modules:
  0.0 150.1 jit_solution(15056490204947444518)
XLA Ops:
  0.0 0.0 copy-start.1
  0.0 0.0 copy-start.2
  0.0 0.0 copy-start.4
  0.0 0.8 broadcast_in_dim.18
  0.8 33.4 %all_to_all.25 = bf16[16,8,512]{2,1,0:T(8,128)(2,1)S(1)} all-to-all(bf16[16,8,512]{2,1,0:T(8,128)(2,1)S(1)} %bitcast.20), channel_id=1, replica_groups=mesh['y'=8,'c'=2,'h'=8,'l'=2,'x'=4] {'c','h'}, dimensions={0} | all-to-all | bytes 262144 | tf_op jit(solution)/shard_map/all_to_all | solution.py:21
  34.2 1.1 broadcast_in_dim.19
  35.3 5.5 %all-to-all-start.1 = ((bf16[8,128,512]{2,1,0:T(8,128)(2,1)}), bf16[8,128,512]{2,1,0:T(8,128)(2,1)S(1)}, u32[]{:S(2)}, u32[]{:S(2)}) async-start(bf16[8,128,512]{2,1,0:T(8,128)(2,1)} %broadcast_in_dim.19), calls=%async_computation.1 | async-start | bytes 2097152 | tf_op jit(solution)/shard_map/all_to_all | solution.py:21
  40.8 0.0 copy-done.1
  40.8 1.9 %collective-permute-start.1 = (bf16[462,512]{1,0:T(8,128)(2,1)S(1)}, bf16[462,512]{1,0:T(8,128)(2,1)S(1)}, u32[]{:S(2)}, u32[]{:S(2)}) collective-permute-start(bf16[462,512]{1,0:T(8,128)(2,1)S(1)} %bitcast.12), channel_id=1, source_target_pairs={{0,64},{64,0},{1,65},{65,1},{2,66},{66,2},{3,67},{67,3},{4,68},{68... | collective-permute-start | bytes 1419272 | tf_op jit(solution)/shard_map/ppermute | solution.py:177
  42.7 0.0 copy-done.2
  42.7 2.4 %collective-permute-start.2 = (bf16[462,512]{1,0:T(8,128)(2,1)S(1)}, bf16[462,512]{1,0:T(8,128)(2,1)S(1)}, u32[]{:S(2)}, u32[]{:S(2)}) collective-permute-start(bf16[462,512]{1,0:T(8,128)(2,1)S(1)} %bitcast.14), channel_id=1, source_target_pairs={{0,64},{64,0},{1,65},{65,1},{2,66},{66,2},{3,67},{67,3},{4,68},{68... | collective-permute-start | bytes 1419272 | tf_op jit(solution)/shard_map/ppermute | solution.py:177
  45.1 0.0 copy-done.4
  45.2 1.9 %collective-permute-start = (f32[1,512]{1,0:T(1,128)S(1)}, f32[1,512]{1,0:T(1,128)S(1)}, u32[]{:S(2)}, u32[]{:S(2)}) collective-permute-start(f32[1,512]{1,0:T(1,128)S(1)} %bitcast.16), channel_id=1, source_target_pairs={{0,64},{64,0},{1,65},{65,1},{2,66},{66,2},{3,67},{67,3},{4,68},{68... | collective-permute-start | bytes 6152 | tf_op jit(solution)/shard_map/ppermute | solution.py:177
  47.1 1.1 collective-permute-done.refs_3_
  48.2 0.0 collective-permute-done.1.refs_4_
  48.2 0.0 collective-permute-done.2.refs_5_
  48.2 6.5 %all-to-all-done.1 = bf16[8,128,512]{2,1,0:T(8,128)(2,1)S(1)} async-done(((bf16[8,128,512]{2,1,0:T(8,128)(2,1)}), bf16[8,128,512]{2,1,0:T(8,128)(2,1)S(1)}, u32[]{:S(2)}, u32[]{:S(2)}) %all-to-all-start.1) | async-done | bytes 1048608 | tf_op jit(solution)/shard_map/all_to_all | solution.py:21
  54.7 2.4 %products.1 = bf16[8,464,128]{2,1,0:T(8,128)(2,1)} custom-call(bf16[8,2,64,512]{3,2,1,0:T(8,128)(2,1)S(1)} %bitcast.10, f32[1,512]{1,0:T(1,128)S(1)} %bitcast.17, bf16[462,512]{1,0:T(8,128)(2,1)S(1)} %bitcast.13, bf16[462,512]{1,0:T(8,128)(2,1)S(1)} %bitcast.15, f32[1,512]{1,0:T(1,128)S(1)} %collective-permute-done.refs_3_, ...), custom_call_target="tpu_custom_call" | custom-call | tf_op jit(solution)/shard_map/products/pallas_call | solution.py:123
  57.1 7.5 %all-to-all-start.2 = ((bf16[8,464,128]{2,1,0:T(8,128)(2,1)}), bf16[8,464,128]{2,1,0:T(8,128)(2,1)S(1)}, u32[]{:S(2)}, u32[]{:S(2)}) async-start(bf16[8,464,128]{2,1,0:T(8,128)(2,1)} %products.1), calls=%async_computation.2 | async-start | bytes 1900544 | tf_op jit(solution)/shard_map/all_to_all | solution.py:21
  64.7 0.0 copy-done.5
  64.7 1.0 copy.8.source_ref
  65.7 1.0 copy-done
  66.8 0.4 pick_rows.1.pick_ref
  67.2 20.8 %all-to-all-done.2.pieces_ref = bf16[8,464,128]{2,1,0:T(8,128)(2,1)S(1)} async-done(((bf16[8,464,128]{2,1,0:T(8,128)(2,1)}), bf16[8,464,128]{2,1,0:T(8,128)(2,1)S(1)}, u32[]{:S(2)}, u32[]{:S(2)}) %all-to-all-start.2) | async-done | bytes 950304 | tf_op jit(solution)/shard_map/all_to_all | solution.py:21
  88.0 0.2 activate.1
  88.2 18.5 %all_gather.3.hidden_ref = bf16[1024,462]{1,0:T(8,128)(2,1)S(1)} all-gather(bf16[64,462]{1,0:T(8,128)(2,1)S(1)} %activate.1), channel_id=1, replica_groups=mesh['y'=8,'c'=2,'h'=8,'l'=2,'x'=4] {'y','c'}, dimensions={0}, use_global_device_ids=true | all-gather | bytes 1005312 | tf_op jit(solution)/shard_map/all_gather | solution.py:180
  106.8 0.0 copy-done.3
  106.8 1.8 %mixed_rows.1 = bf16[1024,512]{1,0:T(8,128)(2,1)S(1)} custom-call(bf16[1024,1024]{1,0:T(8,128)(2,1)S(1)} %pick_rows.1.pick_ref, bf16[1024,462]{1,0:T(8,128)(2,1)S(1)} %all_gather.3.hidden_ref, bf16[462,512]{1,0:T(8,128)(2,1)S(1)} %copy-done.3), custom_call_target="tpu_custom_call" | custom-call | tf_op jit(solution)/shard_map/mixed_rows/pallas_call | solution.py:72
  108.6 21.5 %all_to_all.26 = bf16[8,128,512]{2,1,0:T(8,128)(2,1)S(1)} all-to-all(bf16[8,128,512]{2,1,0:T(8,128)(2,1)S(1)} %bitcast.11), channel_id=1, replica_groups=mesh['y'=8,'c'=2,'h'=8,'l'=2,'x'=4] {'l','x'}, dimensions={0} | all-to-all | bytes 2097152 | tf_op jit(solution)/shard_map/all_to_all | solution.py:21
  130.1 0.1 reduce_sum.24
  130.3 19.2 %all_to_all.27 = bf16[8,16,512]{2,1,0:T(8,128)(2,1)S(1)} all-to-all(bf16[8,16,512]{2,1,0:T(8,128)(2,1)S(1)} %bitcast.19), channel_id=1, replica_groups=mesh['y'=8,'c'=2,'h'=8,'l'=2,'x'=4] {'h'}, dimensions={0} | all-to-all | bytes 262144 | tf_op jit(solution)/shard_map/all_to_all | solution.py:21
  149.5 0.6 reduce_sum.25
  (3 shorter events, 0.0 us)
Async XLA Ops:
  0.0 40.8 %copy-start.1 = (bf16[512,462]{0,1:T(8,128)(2,1)S(1)}, bf16[512,462]{0,1:T(8,128)(2,1)}, u32[]{:S(2)}) copy-start(bf16[512,462]{0,1:T(8,128)(2,1)} %param.9) | copy-start | bytes 1419268
  0.0 42.7 %copy-start.2 = (bf16[512,462]{0,1:T(8,128)(2,1)S(1)}, bf16[512,462]{0,1:T(8,128)(2,1)}, u32[]{:S(2)}) copy-start(bf16[512,462]{0,1:T(8,128)(2,1)} %param.10) | copy-start | bytes 1419268
  0.0 45.1 %copy-start.4 = (f32[512]{0:T(512)S(1)}, f32[512]{0:T(512)}, u32[]{:S(2)}) copy-start(f32[512]{0:T(512)} %param.8) | copy-start | bytes 6148
  35.3 19.4 %all-to-all-start.1 = ((bf16[8,128,512]{2,1,0:T(8,128)(2,1)}), bf16[8,128,512]{2,1,0:T(8,128)(2,1)S(1)}, u32[]{:S(2)}, u32[]{:S(2)}) async-start(bf16[8,128,512]{2,1,0:T(8,128)(2,1)} %broadcast_in_dim.19), calls=%async_computation.1 | async-start | bytes 2097152 | tf_op jit(solution)/shard_map/all_to_all | solution.py:21
  40.8 7.4 %collective-permute-start.1 = (bf16[462,512]{1,0:T(8,128)(2,1)S(1)}, bf16[462,512]{1,0:T(8,128)(2,1)S(1)}, u32[]{:S(2)}, u32[]{:S(2)}) collective-permute-start(bf16[462,512]{1,0:T(8,128)(2,1)S(1)} %bitcast.12), channel_id=1, source_target_pairs={{0,64},{64,0},{1,65},{65,1},{2,66},{66,2},{3,67},{67,3},{4,68},{68... | collective-permute-start | bytes 1419272 | tf_op jit(solution)/shard_map/ppermute | solution.py:177
  42.7 5.5 %collective-permute-start.2 = (bf16[462,512]{1,0:T(8,128)(2,1)S(1)}, bf16[462,512]{1,0:T(8,128)(2,1)S(1)}, u32[]{:S(2)}, u32[]{:S(2)}) collective-permute-start(bf16[462,512]{1,0:T(8,128)(2,1)S(1)} %bitcast.14), channel_id=1, source_target_pairs={{0,64},{64,0},{1,65},{65,1},{2,66},{66,2},{3,67},{67,3},{4,68},{68... | collective-permute-start | bytes 1419272 | tf_op jit(solution)/shard_map/ppermute | solution.py:177
  45.2 3.1 %collective-permute-start = (f32[1,512]{1,0:T(1,128)S(1)}, f32[1,512]{1,0:T(1,128)S(1)}, u32[]{:S(2)}, u32[]{:S(2)}) collective-permute-start(f32[1,512]{1,0:T(1,128)S(1)} %bitcast.16), channel_id=1, source_target_pairs={{0,64},{64,0},{1,65},{65,1},{2,66},{66,2},{3,67},{67,3},{4,68},{68... | collective-permute-start | bytes 6152 | tf_op jit(solution)/shard_map/ppermute | solution.py:177
  54.7 9.9 %copy-start.5 = (s32[1024]{0:T(1024)S(1)}, s32[1024]{0:T(1024)}, u32[]{:S(2)}) copy-start(s32[1024]{0:T(1024)} %param.7) | copy-start | bytes 12292
  57.1 30.9 %all-to-all-start.2 = ((bf16[8,464,128]{2,1,0:T(8,128)(2,1)}), bf16[8,464,128]{2,1,0:T(8,128)(2,1)S(1)}, u32[]{:S(2)}, u32[]{:S(2)}) async-start(bf16[8,464,128]{2,1,0:T(8,128)(2,1)} %products.1), calls=%async_computation.2 | async-start | bytes 1900544 | tf_op jit(solution)/shard_map/all_to_all | solution.py:21
  65.7 1.0 copy-start
  66.8 40.0 %copy-start.3 = (bf16[462,512]{1,0:T(8,128)(2,1)S(1)}, bf16[462,512]{1,0:T(8,128)(2,1)}, u32[]{:S(2)}) copy-start(bf16[462,512]{1,0:T(8,128)(2,1)} %down_ref.1) | copy-start | bytes 1419268

commit v7 on v6

--- a/solution.py
+++ b/solution.py
@@ -172,13 +172,15 @@
     sizes = (ny, nc, nh, nl, nx, share)
     halves = jnp.broadcast_to(tokens.reshape(nc, 1, part, depth), (nc, nh, part, depth))
     halves = swapped(halves.reshape(nc * nh, part, depth), ("c", "h")).reshape(-1, depth)
-    gathered = copied_to_all(halves, NEAR).reshape(nl * nx, nc, nh * part, depth)
     own = (gain[None, :], gate_weight.T, up_weight.T)
     other = [lax.ppermute(v, "c", [(0, 1), (1, 0)]) for v in own]
+    early = (halves, pick_rows(sizes, source), other)
+    halves, pick, other = lax.optimization_barrier(early)
+    gathered = copied_to_all(halves, NEAR).reshape(nl * nx, nc, nh * part, depth)
     pieces = swapped(products(ny, gathered, *own, *other), "y")
     hidden = activate(pieces, units, nl * nx * nh * part // ny)
     hidden = lax.all_gather(hidden, ("y", "c"), axis=0, tiled=True)
-    mixed = mixed_rows(pick_rows(sizes, source), hidden, down_weight)
+    mixed = mixed_rows(pick, hidden, down_weight)
     mixed = summed(swapped(mixed.reshape(nl * nx, -1, depth), NEAR))
     return summed(swapped(mixed.reshape(nh, share, depth), "h"))
 

time: 151 us -> 152 us (level)
  waiting for transfers between devices: 28.5 us -> 6.8 us
  blocking collectives: 92.7 us -> 110 us
  starting transfers between devices: 19.3 us -> 25.5 us
    all_to_all x2 -> x1, waiting for transfers between devices: 27.3 us -> 6.79 us  [swapped(): return lax.all_to_all(value, axis, split_axis=0, concat_axis=0, tiled=True)]
    all_to_all x3 -> x4, blocking collectives: 74.2 us -> 91.9 us  [swapped(): return lax.all_to_all(value, axis, split_axis=0, concat_axis=0, tiled=True)]
    all_to_all x2 -> x1, starting transfers between devices: 13 us -> 18.9 us  [swapped(): return lax.all_to_all(value, axis, split_axis=0, concat_axis=0, tiled=True)]
  transfers between devices with their start and end apart: 5 -> 4, of which waited for: 3 -> 1; matrix products, arithmetic and copies ran while one was open for 1% -> 1% of each run, Pallas kernels for 0% -> 0%
where the time goes in v7:
time: 152 us
  blocking collectives  110 us (72%)
  starting transfers between devices  25.5 us (17%)
  waiting for transfers between devices  6.8 us (4%)
  Pallas kernels  4.87 us (3%)
  local copies, waits for them, and re-layouts  3.29 us (2%)
    all_to_all x4, blocking collectives, swapped(): return lax.all_to_all(value, axis, split_axis=0, concat_axis=0, tiled=True)  91.9 us
    all_to_all x1, starting transfers between devices, swapped(): return lax.all_to_all(value, axis, split_axis=0, concat_axis=0, tiled=True)  18.9 us
    all_gather x1, blocking collectives, on_device(): hidden = lax.all_gather(hidden, ('y', 'c'), axis=0, tiled=True)  18.5 us
    all_to_all x1, waiting for transfers between devices, swapped(): return lax.all_to_all(value, axis, split_axis=0, concat_axis=0, tiled=True)  6.79 us
    ppermute x3, starting transfers between devices, on_device(): other = [lax.ppermute(v, 'c', [(0, 1), (1, 0)]) for v in own]  6.59 us
  transfers between devices with their start and end apart: 4, of which 1 were waited for; matrix products, arithmetic and copies ran while one was open for 1% of the time, Pallas kernels for 0%

profile of v7, /device:TPU:8, one launch (start us, length us, event | category | flops | bytes accessed | tf_op | source)
XLA Modules:
  0.0 151.8 jit_solution(16709078480070171502)
XLA Ops:
  0.0 1.4 broadcast_in_dim.17
  1.4 18.9 %all-to-all-start = ((bf16[16,8,512]{2,1,0:T(8,128)(2,1)}), bf16[16,8,512]{2,1,0:T(8,128)(2,1)}, u32[]{:S(2)}, u32[]{:S(2)}) async-start(bf16[16,8,512]{2,1,0:T(8,128)(2,1)} %bitcast.1), calls=%async_computation | async-start | bytes 262144 | tf_op jit(solution)/shard_map/all_to_all | solution.py:21
  20.3 2.3 %collective-permute-start.1 = (bf16[462,512]{1,0:T(8,128)(2,1)}, bf16[462,512]{1,0:T(8,128)(2,1)S(1)}, u32[]{:S(2)}, u32[]{:S(2)}) collective-permute-start(bf16[462,512]{1,0:T(8,128)(2,1)} %bitcast.12), channel_id=1, source_target_pairs={{0,64},{64,0},{1,65},{65,1},{2,66},{66,2},{3,67},{67,3},{4,68},{68... | collective-permute-start | bytes 1419272 | tf_op jit(solution)/shard_map/ppermute | solution.py:176
  22.6 2.1 %collective-permute-start.2 = (bf16[462,512]{1,0:T(8,128)(2,1)}, bf16[462,512]{1,0:T(8,128)(2,1)}, u32[]{:S(2)}, u32[]{:S(2)}) collective-permute-start(bf16[462,512]{1,0:T(8,128)(2,1)} %bitcast.14), channel_id=1, source_target_pairs={{0,64},{64,0},{1,65},{65,1},{2,66},{66,2},{3,67},{67,3},{4,68},{68... | collective-permute-start | bytes 1419272 | tf_op jit(solution)/shard_map/ppermute | solution.py:176
  24.6 2.3 %collective-permute-start = (f32[1,512]{1,0:T(1,128)}, f32[1,512]{1,0:T(1,128)S(1)}, u32[]{:S(2)}, u32[]{:S(2)}) collective-permute-start(f32[1,512]{1,0:T(1,128)} %bitcast.16), channel_id=1, source_target_pairs={{0,64},{64,0},{1,65},{65,1},{2,66},{66,2},{3,67},{67,3},{4,68},{68... | collective-permute-start | bytes 6152 | tf_op jit(solution)/shard_map/ppermute | solution.py:176
  26.9 0.9 copy.8.source_ref
  27.8 0.4 pick_rows.1.pick_ref
  28.3 0.0 copy-start
  28.3 0.0 copy-start.1
  28.3 0.0 copy-start.3
  28.3 0.0 collective-permute-done.refs_3_
  28.3 0.0 collective-permute-done.1.refs_4_
  28.3 0.0 collective-permute-done.2.refs_5_
  28.3 6.8 %all-to-all-done = bf16[16,8,512]{2,1,0:T(8,128)(2,1)} async-done(((bf16[16,8,512]{2,1,0:T(8,128)(2,1)}), bf16[16,8,512]{2,1,0:T(8,128)(2,1)}, u32[]{:S(2)}, u32[]{:S(2)}) %all-to-all-start) | async-done | bytes 131104 | tf_op jit(solution)/shard_map/all_to_all | solution.py:21
  35.1 1.0 broadcast_in_dim.20
  36.1 20.1 %all_to_all.25 = bf16[8,128,512]{2,1,0:T(8,128)(2,1)S(1)} all-to-all(bf16[8,128,512]{2,1,0:T(8,128)(2,1)S(1)} %broadcast_in_dim.20), channel_id=1, replica_groups=mesh['y'=8,'c'=2,'h'=8,'l'=2,'x'=4] {'l','x'}, dimensions={0} | all-to-all | bytes 2097152 | tf_op jit(solution)/shard_map/all_to_all | solution.py:21
  56.2 0.0 copy-done
  56.2 0.0 copy-done.1
  56.2 0.0 copy-done.3
  56.2 2.5 %products.1 = bf16[8,464,128]{2,1,0:T(8,128)(2,1)S(1)} custom-call(bf16[8,2,64,512]{3,2,1,0:T(8,128)(2,1)S(1)} %bitcast.10, f32[1,512]{1,0:T(1,128)S(1)} %bitcast.17, bf16[462,512]{1,0:T(8,128)(2,1)S(1)} %bitcast.13, bf16[462,512]{1,0:T(8,128)(2,1)S(1)} %bitcast.15, f32[1,512]{1,0:T(1,128)S(1)} %collective-permute-done.refs_3_, ...), custom_call_target="tpu_custom_call" | custom-call | tf_op jit(solution)/shard_map/products/pallas_call | solution.py:123
  58.6 0.0 copy-start.2
  58.6 29.7 %all_to_all.26.pieces_ref = bf16[8,464,128]{2,1,0:T(8,128)(2,1)S(1)} all-to-all(bf16[8,464,128]{2,1,0:T(8,128)(2,1)S(1)} %products.1), channel_id=1, replica_groups=mesh['y'=8,'c'=2,'h'=8,'l'=2,'x'=4] {'y'}, dimensions={0} | all-to-all | bytes 1900544 | tf_op jit(solution)/shard_map/all_to_all | solution.py:21
  88.4 0.2 activate.1
  88.6 18.5 %all_gather.3.hidden_ref = bf16[1024,462]{1,0:T(8,128)(2,1)S(1)} all-gather(bf16[64,462]{1,0:T(8,128)(2,1)S(1)} %activate.1), channel_id=1, replica_groups=mesh['y'=8,'c'=2,'h'=8,'l'=2,'x'=4] {'y','c'}, dimensions={0}, use_global_device_ids=true | all-gather | bytes 1005312 | tf_op jit(solution)/shard_map/all_gather | solution.py:182
  107.1 0.0 copy-done.2
  107.1 1.8 %mixed_rows.1 = bf16[1024,512]{1,0:T(8,128)(2,1)S(1)} custom-call(bf16[1024,1024]{1,0:T(8,128)(2,1)S(1)} %pick_rows.1.pick_ref, bf16[1024,462]{1,0:T(8,128)(2,1)S(1)} %all_gather.3.hidden_ref, bf16[462,512]{1,0:T(8,128)(2,1)S(1)} %copy-done.2), custom_call_target="tpu_custom_call" | custom-call | tf_op jit(solution)/shard_map/mixed_rows/pallas_call | solution.py:72
  108.9 20.3 %all_to_all.27 = bf16[8,128,512]{2,1,0:T(8,128)(2,1)S(1)} all-to-all(bf16[8,128,512]{2,1,0:T(8,128)(2,1)S(1)} %bitcast.11), channel_id=1, replica_groups=mesh['y'=8,'c'=2,'h'=8,'l'=2,'x'=4] {'l','x'}, dimensions={0} | all-to-all | bytes 2097152 | tf_op jit(solution)/shard_map/all_to_all | solution.py:21
  129.3 0.1 reduce_sum.24
  129.4 21.7 %all_to_all.28 = bf16[8,16,512]{2,1,0:T(8,128)(2,1)S(1)} all-to-all(bf16[8,16,512]{2,1,0:T(8,128)(2,1)S(1)} %bitcast.18), channel_id=1, replica_groups=mesh['y'=8,'c'=2,'h'=8,'l'=2,'x'=4] {'h'}, dimensions={0} | all-to-all | bytes 262144 | tf_op jit(solution)/shard_map/all_to_all | solution.py:21
  151.1 0.6 reduce_sum.25
Async XLA Ops:
  1.4 33.7 %all-to-all-start = ((bf16[16,8,512]{2,1,0:T(8,128)(2,1)}), bf16[16,8,512]{2,1,0:T(8,128)(2,1)}, u32[]{:S(2)}, u32[]{:S(2)}) async-start(bf16[16,8,512]{2,1,0:T(8,128)(2,1)} %bitcast.1), calls=%async_computation | async-start | bytes 262144 | tf_op jit(solution)/shard_map/all_to_all | solution.py:21
  20.3 8.0 %collective-permute-start.1 = (bf16[462,512]{1,0:T(8,128)(2,1)}, bf16[462,512]{1,0:T(8,128)(2,1)S(1)}, u32[]{:S(2)}, u32[]{:S(2)}) collective-permute-start(bf16[462,512]{1,0:T(8,128)(2,1)} %bitcast.12), channel_id=1, source_target_pairs={{0,64},{64,0},{1,65},{65,1},{2,66},{66,2},{3,67},{67,3},{4,68},{68... | collective-permute-start | bytes 1419272 | tf_op jit(solution)/shard_map/ppermute | solution.py:176
  22.6 5.8 %collective-permute-start.2 = (bf16[462,512]{1,0:T(8,128)(2,1)}, bf16[462,512]{1,0:T(8,128)(2,1)}, u32[]{:S(2)}, u32[]{:S(2)}) collective-permute-start(bf16[462,512]{1,0:T(8,128)(2,1)} %bitcast.14), channel_id=1, source_target_pairs={{0,64},{64,0},{1,65},{65,1},{2,66},{66,2},{3,67},{67,3},{4,68},{68... | collective-permute-start | bytes 1419272 | tf_op jit(solution)/shard_map/ppermute | solution.py:176
  24.6 3.7 %collective-permute-start = (f32[1,512]{1,0:T(1,128)}, f32[1,512]{1,0:T(1,128)S(1)}, u32[]{:S(2)}, u32[]{:S(2)}) collective-permute-start(f32[1,512]{1,0:T(1,128)} %bitcast.16), channel_id=1, source_target_pairs={{0,64},{64,0},{1,65},{65,1},{2,66},{66,2},{3,67},{67,3},{4,68},{68... | collective-permute-start | bytes 6152 | tf_op jit(solution)/shard_map/ppermute | solution.py:176
  28.3 27.9 %copy-start = (bf16[512,462]{0,1:T(8,128)(2,1)S(1)}, bf16[512,462]{0,1:T(8,128)(2,1)}, u32[]{:S(2)}) copy-start(bf16[512,462]{0,1:T(8,128)(2,1)} %param.9) | copy-start | bytes 1419268
  28.3 27.9 %copy-start.1 = (bf16[512,462]{0,1:T(8,128)(2,1)S(1)}, bf16[512,462]{0,1:T(8,128)(2,1)}, u32[]{:S(2)}) copy-start(bf16[512,462]{0,1:T(8,128)(2,1)} %param.10) | copy-start | bytes 1419268
  28.3 27.9 %copy-start.3 = (f32[512]{0:T(512)S(1)}, f32[512]{0:T(512)}, u32[]{:S(2)}) copy-start(f32[512]{0:T(512)} %param.8) | copy-start | bytes 6148
  58.6 48.5 %copy-start.2 = (bf16[462,512]{1,0:T(8,128)(2,1)S(1)}, bf16[462,512]{1,0:T(8,128)(2,1)}, u32[]{:S(2)}) copy-start(bf16[462,512]{1,0:T(8,128)(2,1)} %down_ref.1) | copy-start | bytes 1419268

commit v8 on v6

--- a/solution.py
+++ b/solution.py
@@ -81,21 +81,23 @@
 
 
 def products_kernel(gathered_ref, *refs):
-    sides, (out_ref, weight_ref) = (refs[:3], refs[3:6]), refs[6:]
+    sides, (out_ref, row_ref, gate_all, up_all) = (refs[:3], refs[3:6]), refs[6:]
     ny, depth, units = out_ref.shape[0], gathered_ref.shape[3], refs[1].shape[0]
     kept = gathered_ref.shape[0] * gathered_ref.shape[2]
     block = kept // ny
-    weight_ref[units:, :] = jnp.zeros((weight_ref.shape[0] - units, depth), jnp.bfloat16)
     core = lax.axis_index("c")
-    squares, gate, up = 0.0, 0.0, 0.0
-    for side, (gain_ref, gate_ref, up_ref) in zip((core, 1 - core), sides):
+    squares = 0.0
+    for k, (gain_ref, gate_ref, up_ref) in enumerate(sides):
+        at = k * depth
+        side = core if k == 0 else 1 - core
+        for weight_ref, all_ref in ((gate_ref, gate_all), (up_ref, up_all)):
+            all_ref[units:, at : at + depth] = jnp.zeros((all_ref.shape[0] - units, depth), jnp.bfloat16)
+            all_ref[:units, at : at + depth] = weight_ref[...]
         merged = gathered_ref[:, pl.ds(side, 1)].astype(jnp.float32).reshape(kept, depth)
         squares += jnp.sum(merged * merged, axis=1, keepdims=True)
-        weighted = (merged * gain_ref[...]).astype(jnp.bfloat16)
-        weight_ref[:units, :] = gate_ref[...]
-        gate += lax.dot_general(weighted, weight_ref[...], NT, preferred_element_type=jnp.float32)
-        weight_ref[:units, :] = up_ref[...]
-        up += lax.dot_general(weighted, weight_ref[...], NT, preferred_element_type=jnp.float32)
+        row_ref[:, at : at + depth] = (merged * gain_ref[...]).astype(jnp.bfloat16)
+    gate = lax.dot_general(row_ref[...], gate_all[...], NT, preferred_element_type=jnp.float32)
+    up = lax.dot_general(row_ref[...], up_all[...], NT, preferred_element_type=jnp.float32)
     full, tail = units // LANES, units % LANES
     over = 2 * tail - LANES
     rolled = pltpu.roll(up[:, full * LANES :], tail, 1)
@@ -125,7 +127,11 @@
         out_shape=jax.ShapeDtypeStruct((ny, rows, LANES), jnp.bfloat16),
         in_specs=[VM] * 7,
         out_specs=VM,
-        scratch_shapes=[pltpu.VMEM(((full + 1) * LANES, depth), jnp.bfloat16)],
+        scratch_shapes=[
+            pltpu.VMEM((block * ny, 2 * depth), jnp.bfloat16),
+            pltpu.VMEM(((full + 1) * LANES, 2 * depth), jnp.bfloat16),
+            pltpu.VMEM(((full + 1) * LANES, 2 * depth), jnp.bfloat16),
+        ],
         interpret=INTERPRET,
         compiler_params=pltpu.CompilerParams(vmem_limit_bytes=24 << 20),
         name="products",
@@ -175,10 +181,11 @@
     gathered = copied_to_all(halves, NEAR).reshape(nl * nx, nc, nh * part, depth)
     own = (gain[None, :], gate_weight.T, up_weight.T)
     other = [lax.ppermute(v, "c", [(0, 1), (1, 0)]) for v in own]
+    pick = pick_rows(sizes, source)
     pieces = swapped(products(ny, gathered, *own, *other), "y")
     hidden = activate(pieces, units, nl * nx * nh * part // ny)
     hidden = lax.all_gather(hidden, ("y", "c"), axis=0, tiled=True)
-    mixed = mixed_rows(pick_rows(sizes, source), hidden, down_weight)
+    mixed = mixed_rows(pick, hidden, down_weight)
     mixed = summed(swapped(mixed.reshape(nl * nx, -1, depth), NEAR))
     return summed(swapped(mixed.reshape(nh, share, depth), "h"))
 

time: 151 us -> 151 us (level)
  no operation moved by 1% of the time
where the time goes in v8:
time: 151 us; the launch traced here: 150 us
  blocking collectives  92.7 us (61%)
  waiting for transfers between devices  28.5 us (19%)
  starting transfers between devices  19.3 us (13%)
  Pallas kernels  4.82 us (3%)
  local copies, waits for them, and re-layouts  3.96 us (3%)
    all_to_all x3, blocking collectives, swapped(): return lax.all_to_all(value, axis, split_axis=0, concat_axis=0, tiled=True)  74.2 us
    all_to_all x2, waiting for transfers between devices, swapped(): return lax.all_to_all(value, axis, split_axis=0, concat_axis=0, tiled=True)  27.3 us
    all_gather x1, blocking collectives, on_device(): hidden = lax.all_gather(hidden, ('y', 'c'), axis=0, tiled=True)  18.5 us
    all_to_all x2, starting transfers between devices, swapped(): return lax.all_to_all(value, axis, split_axis=0, concat_axis=0, tiled=True)  13 us
    ppermute x3, starting transfers between devices, on_device(): other = [lax.ppermute(v, 'c', [(0, 1), (1, 0)]) for v in own]  6.25 us
  transfers between devices with their start and end apart: 5, of which 3 were waited for; matrix products, arithmetic and copies ran while one was open for 1% of the time, Pallas kernels for 0%

profile of v8, /device:TPU:8, one launch (start us, length us, event | category | flops | bytes accessed | tf_op | source)
XLA Modules:
  0.0 150.1 jit_solution(16498215874090302677)
XLA Ops:
  0.0 0.0 copy-start.1
  0.0 0.0 copy-start.2
  0.0 0.0 copy-start.4
  0.0 0.8 broadcast_in_dim.18
  0.8 33.4 %all_to_all.25 = bf16[16,8,512]{2,1,0:T(8,128)(2,1)S(1)} all-to-all(bf16[16,8,512]{2,1,0:T(8,128)(2,1)S(1)} %bitcast.20), channel_id=1, replica_groups=mesh['y'=8,'c'=2,'h'=8,'l'=2,'x'=4] {'c','h'}, dimensions={0} | all-to-all | bytes 262144 | tf_op jit(solution)/shard_map/all_to_all | solution.py:21
  34.2 1.1 broadcast_in_dim.19
  35.3 5.5 %all-to-all-start.1 = ((bf16[8,128,512]{2,1,0:T(8,128)(2,1)}), bf16[8,128,512]{2,1,0:T(8,128)(2,1)S(1)}, u32[]{:S(2)}, u32[]{:S(2)}) async-start(bf16[8,128,512]{2,1,0:T(8,128)(2,1)} %broadcast_in_dim.19), calls=%async_computation.1 | async-start | bytes 2097152 | tf_op jit(solution)/shard_map/all_to_all | solution.py:21
  40.8 0.0 copy-done.1
  40.8 1.9 %collective-permute-start.1 = (bf16[462,512]{1,0:T(8,128)(2,1)S(1)}, bf16[462,512]{1,0:T(8,128)(2,1)S(1)}, u32[]{:S(2)}, u32[]{:S(2)}) collective-permute-start(bf16[462,512]{1,0:T(8,128)(2,1)S(1)} %bitcast.12), channel_id=1, source_target_pairs={{0,64},{64,0},{1,65},{65,1},{2,66},{66,2},{3,67},{67,3},{4,68},{68... | collective-permute-start | bytes 1419272 | tf_op jit(solution)/shard_map/ppermute | solution.py:183
  42.7 0.0 copy-done.2
  42.7 2.4 %collective-permute-start.2 = (bf16[462,512]{1,0:T(8,128)(2,1)S(1)}, bf16[462,512]{1,0:T(8,128)(2,1)S(1)}, u32[]{:S(2)}, u32[]{:S(2)}) collective-permute-start(bf16[462,512]{1,0:T(8,128)(2,1)S(1)} %bitcast.14), channel_id=1, source_target_pairs={{0,64},{64,0},{1,65},{65,1},{2,66},{66,2},{3,67},{67,3},{4,68},{68... | collective-permute-start | bytes 1419272 | tf_op jit(solution)/shard_map/ppermute | solution.py:183
  45.1 0.0 copy-done.4
  45.2 1.9 %collective-permute-start = (f32[1,512]{1,0:T(1,128)S(1)}, f32[1,512]{1,0:T(1,128)S(1)}, u32[]{:S(2)}, u32[]{:S(2)}) collective-permute-start(f32[1,512]{1,0:T(1,128)S(1)} %bitcast.16), channel_id=1, source_target_pairs={{0,64},{64,0},{1,65},{65,1},{2,66},{66,2},{3,67},{67,3},{4,68},{68... | collective-permute-start | bytes 6152 | tf_op jit(solution)/shard_map/ppermute | solution.py:183
  47.1 1.1 collective-permute-done.refs_3_
  48.2 0.0 collective-permute-done.1.refs_4_
  48.2 0.0 collective-permute-done.2.refs_5_
  48.2 6.5 %all-to-all-done.1 = bf16[8,128,512]{2,1,0:T(8,128)(2,1)S(1)} async-done(((bf16[8,128,512]{2,1,0:T(8,128)(2,1)}), bf16[8,128,512]{2,1,0:T(8,128)(2,1)S(1)}, u32[]{:S(2)}, u32[]{:S(2)}) %all-to-all-start.1) | async-done | bytes 1048608 | tf_op jit(solution)/shard_map/all_to_all | solution.py:21
  54.7 2.4 %products.1 = bf16[8,464,128]{2,1,0:T(8,128)(2,1)} custom-call(bf16[8,2,64,512]{3,2,1,0:T(8,128)(2,1)S(1)} %bitcast.10, f32[1,512]{1,0:T(1,128)S(1)} %bitcast.17, bf16[462,512]{1,0:T(8,128)(2,1)S(1)} %bitcast.13, bf16[462,512]{1,0:T(8,128)(2,1)S(1)} %bitcast.15, f32[1,512]{1,0:T(1,128)S(1)} %collective-permute-done.refs_3_, ...), custom_call_target="tpu_custom_call" | custom-call | tf_op jit(solution)/shard_map/products/pallas_call | solution.py:125
  57.1 7.5 %all-to-all-start.2 = ((bf16[8,464,128]{2,1,0:T(8,128)(2,1)}), bf16[8,464,128]{2,1,0:T(8,128)(2,1)S(1)}, u32[]{:S(2)}, u32[]{:S(2)}) async-start(bf16[8,464,128]{2,1,0:T(8,128)(2,1)} %products.1), calls=%async_computation.2 | async-start | bytes 1900544 | tf_op jit(solution)/shard_map/all_to_all | solution.py:21
  64.7 0.0 copy-done.5
  64.7 1.0 copy.8.source_ref
  65.7 1.0 copy-done
  66.8 0.4 pick_rows.1.pick_ref
  67.2 20.8 %all-to-all-done.2.pieces_ref = bf16[8,464,128]{2,1,0:T(8,128)(2,1)S(1)} async-done(((bf16[8,464,128]{2,1,0:T(8,128)(2,1)}), bf16[8,464,128]{2,1,0:T(8,128)(2,1)S(1)}, u32[]{:S(2)}, u32[]{:S(2)}) %all-to-all-start.2) | async-done | bytes 950304 | tf_op jit(solution)/shard_map/all_to_all | solution.py:21
  88.0 0.2 activate.1
  88.2 18.5 %all_gather.3.hidden_ref = bf16[1024,462]{1,0:T(8,128)(2,1)S(1)} all-gather(bf16[64,462]{1,0:T(8,128)(2,1)S(1)} %activate.1), channel_id=1, replica_groups=mesh['y'=8,'c'=2,'h'=8,'l'=2,'x'=4] {'y','c'}, dimensions={0}, use_global_device_ids=true | all-gather | bytes 1005312 | tf_op jit(solution)/shard_map/all_gather | solution.py:187
  106.8 0.0 copy-done.3
  106.8 1.8 %mixed_rows.1 = bf16[1024,512]{1,0:T(8,128)(2,1)S(1)} custom-call(bf16[1024,1024]{1,0:T(8,128)(2,1)S(1)} %pick_rows.1.pick_ref, bf16[1024,462]{1,0:T(8,128)(2,1)S(1)} %all_gather.3.hidden_ref, bf16[462,512]{1,0:T(8,128)(2,1)S(1)} %copy-done.3), custom_call_target="tpu_custom_call" | custom-call | tf_op jit(solution)/shard_map/mixed_rows/pallas_call | solution.py:72
  108.6 21.5 %all_to_all.26 = bf16[8,128,512]{2,1,0:T(8,128)(2,1)S(1)} all-to-all(bf16[8,128,512]{2,1,0:T(8,128)(2,1)S(1)} %bitcast.11), channel_id=1, replica_groups=mesh['y'=8,'c'=2,'h'=8,'l'=2,'x'=4] {'l','x'}, dimensions={0} | all-to-all | bytes 2097152 | tf_op jit(solution)/shard_map/all_to_all | solution.py:21
  130.1 0.1 reduce_sum.24
  130.3 19.2 %all_to_all.27 = bf16[8,16,512]{2,1,0:T(8,128)(2,1)S(1)} all-to-all(bf16[8,16,512]{2,1,0:T(8,128)(2,1)S(1)} %bitcast.19), channel_id=1, replica_groups=mesh['y'=8,'c'=2,'h'=8,'l'=2,'x'=4] {'h'}, dimensions={0} | all-to-all | bytes 262144 | tf_op jit(solution)/shard_map/all_to_all | solution.py:21
  149.4 0.6 reduce_sum.25
  (3 shorter events, 0.0 us)
Async XLA Ops:
  0.0 40.8 %copy-start.1 = (bf16[512,462]{0,1:T(8,128)(2,1)S(1)}, bf16[512,462]{0,1:T(8,128)(2,1)}, u32[]{:S(2)}) copy-start(bf16[512,462]{0,1:T(8,128)(2,1)} %param.9) | copy-start | bytes 1419268
  0.0 42.7 %copy-start.2 = (bf16[512,462]{0,1:T(8,128)(2,1)S(1)}, bf16[512,462]{0,1:T(8,128)(2,1)}, u32[]{:S(2)}) copy-start(bf16[512,462]{0,1:T(8,128)(2,1)} %param.10) | copy-start | bytes 1419268
  0.0 45.1 %copy-start.4 = (f32[512]{0:T(512)S(1)}, f32[512]{0:T(512)}, u32[]{:S(2)}) copy-start(f32[512]{0:T(512)} %param.8) | copy-start | bytes 6148
  35.3 19.4 %all-to-all-start.1 = ((bf16[8,128,512]{2,1,0:T(8,128)(2,1)}), bf16[8,128,512]{2,1,0:T(8,128)(2,1)S(1)}, u32[]{:S(2)}, u32[]{:S(2)}) async-start(bf16[8,128,512]{2,1,0:T(8,128)(2,1)} %broadcast_in_dim.19), calls=%async_computation.1 | async-start | bytes 2097152 | tf_op jit(solution)/shard_map/all_to_all | solution.py:21
  40.8 7.4 %collective-permute-start.1 = (bf16[462,512]{1,0:T(8,128)(2,1)S(1)}, bf16[462,512]{1,0:T(8,128)(2,1)S(1)}, u32[]{:S(2)}, u32[]{:S(2)}) collective-permute-start(bf16[462,512]{1,0:T(8,128)(2,1)S(1)} %bitcast.12), channel_id=1, source_target_pairs={{0,64},{64,0},{1,65},{65,1},{2,66},{66,2},{3,67},{67,3},{4,68},{68... | collective-permute-start | bytes 1419272 | tf_op jit(solution)/shard_map/ppermute | solution.py:183
  42.7 5.5 %collective-permute-start.2 = (bf16[462,512]{1,0:T(8,128)(2,1)S(1)}, bf16[462,512]{1,0:T(8,128)(2,1)S(1)}, u32[]{:S(2)}, u32[]{:S(2)}) collective-permute-start(bf16[462,512]{1,0:T(8,128)(2,1)S(1)} %bitcast.14), channel_id=1, source_target_pairs={{0,64},{64,0},{1,65},{65,1},{2,66},{66,2},{3,67},{67,3},{4,68},{68... | collective-permute-start | bytes 1419272 | tf_op jit(solution)/shard_map/ppermute | solution.py:183
  45.2 3.1 %collective-permute-start = (f32[1,512]{1,0:T(1,128)S(1)}, f32[1,512]{1,0:T(1,128)S(1)}, u32[]{:S(2)}, u32[]{:S(2)}) collective-permute-start(f32[1,512]{1,0:T(1,128)S(1)} %bitcast.16), channel_id=1, source_target_pairs={{0,64},{64,0},{1,65},{65,1},{2,66},{66,2},{3,67},{67,3},{4,68},{68... | collective-permute-start | bytes 6152 | tf_op jit(solution)/shard_map/ppermute | solution.py:183
  54.7 9.9 %copy-start.5 = (s32[1024]{0:T(1024)S(1)}, s32[1024]{0:T(1024)}, u32[]{:S(2)}) copy-start(s32[1024]{0:T(1024)} %param.7) | copy-start | bytes 12292
  57.1 30.9 %all-to-all-start.2 = ((bf16[8,464,128]{2,1,0:T(8,128)(2,1)}), bf16[8,464,128]{2,1,0:T(8,128)(2,1)S(1)}, u32[]{:S(2)}, u32[]{:S(2)}) async-start(bf16[8,464,128]{2,1,0:T(8,128)(2,1)} %products.1), calls=%async_computation.2 | async-start | bytes 1900544 | tf_op jit(solution)/shard_map/all_to_all | solution.py:21
  65.7 1.0 copy-start
  66.8 40.0 %copy-start.3 = (bf16[462,512]{1,0:T(8,128)(2,1)S(1)}, bf16[462,512]{1,0:T(8,128)(2,1)}, u32[]{:S(2)}) copy-start(bf16[462,512]{1,0:T(8,128)(2,1)} %down_ref.1) | copy-start | bytes 1419268
